TPU v7x, 512 devices: a whole 4x4x16 slice. The times are simulated.
512 devices in a mesh: ctx: 32 (over y_lo, z), grp: 16 (over y_hi, x, core).
Axes of the slice: x: 4, y: 4 (y_hi: 2, y_lo: 2; y = y_hi * 2 + y_lo), z: 16, core: 2. Of those that a mesh axis runs over, the one named last changes fastest.
Arguments:
- queries: bfloat16 [16, 16384, 512], P('grp', 'ctx'), as said below
- keys: bfloat16 [16, 16384, 512], P('grp', 'ctx'), as said below
- values: bfloat16 [16, 16384, 512], P('grp', 'ctx'), may hold values from -6 to 6
- summary_pos: int32 [16, 32, 8], P('grp', 'ctx'), may hold values from 0 to 511, as said below
Outputs:
- attended: bfloat16 [16, 16384, 512], P('grp', 'ctx')
Inputs may be any that keep to these rules, and one draw needn't show every extreme that they name: queries' entries lie within -320 and 320. keys' entries lie within -6 and 6. `summary_pos`: in each block the j-th summary position lies in [j * 64, (j + 1) * 64); the last one is 511.
All inputs are finite; a program needn't handle non-finite values.
Results may differ from a plain program's by a relative error of at most 0.0045.
Values may be sent and summed in bfloat16 or wider, within the bound.
No kernel may reach another device: no remote copies, remote signals or barrier semaphores. Data moves between devices by JAX's collectives and lax.ppermute only.
A program may use at most 64 MiB of HBM per device.

v0:
```python
import math

import jax
import jax.numpy as jnp
from jax import lax
from jax.sharding import PartitionSpec as P

H = 8
HD = 64
BLK = 512
SUMM = 8


masked_score = -1e30


def shifted(value, axis, steps):
    count = lax.axis_size(axis)
    pairs = [(source, (source + steps) % count) for source in range(count)]
    return lax.ppermute(value, axis, pairs)


def shifted_2(value, axis, by):
    count = lax.axis_size(axis)
    pairs = [(i, i + by) for i in range(count) if 0 <= i + by < count]
    return lax.ppermute(value, axis, pairs)


def copy_for_each(value, axis):
    copies = jnp.broadcast_to(value, (lax.axis_size(axis), *value.shape))
    return lax.all_to_all(copies, axis, split_axis=0, concat_axis=0, tiled=True)


def in_order(pieces, dim):
    dims = list(pieces.shape[1:])
    dims[dim] *= pieces.shape[0]
    return jnp.moveaxis(pieces, 0, dim).reshape(dims)


def gathered_copies(value, axis, dim):
    pieces = copy_for_each(value, axis)
    return in_order(pieces, dim)


def fold_rows(running, qheads, qblock, summary_rows, row_block, score_scale):
    half_width = summary_rows.shape[1] // 2
    head_count = running[0].shape[0]
    head_size = half_width // head_count

    def update(current, tile_pair):
        piece_rows, blocks = tile_pair
        peak_old, total_old, summed_old = current
        tile_keys = piece_rows[:, :half_width].reshape(-1, head_count, head_size)
        tile_vals = piece_rows[:, half_width:].reshape(-1, head_count, head_size)
        scores = (
            jnp.einsum("qhd,rhd->hqr", qheads, tile_keys, preferred_element_type=jnp.float32)
            * score_scale
        )
        allowed = (blocks[None, :] <= qblock[:, None] - 2)[None]
        scores = jnp.where(allowed, scores, masked_score)
        higher = jnp.maximum(peak_old, scores.max(-1))
        weights = jnp.where(allowed, jnp.exp(scores - higher[..., None]), 0.0)
        rescale = jnp.exp(peak_old - higher)
        total_new = total_old * rescale + weights.sum(-1)
        summed_new = summed_old * rescale[..., None] + jnp.einsum(
            "hqr,rhd->hqd",
            weights.astype(jnp.bfloat16),
            tile_vals,
            preferred_element_type=jnp.float32,
        )
        return ((higher, total_new, summed_new), None)

    row_count = summary_rows.shape[0]
    tile_list = (
        summary_rows.reshape(row_count // 512, 512, -1),
        row_block.reshape(row_count // 512, 512),
    )
    result, unused = lax.scan(update, running, tile_list)
    return result


def shards(queries, keys, values, summary_pos):
    ctx_count = lax.axis_size("ctx")
    ctx_index = lax.axis_index("ctx")
    grp_index = lax.axis_index("grp")
    device_flat = grp_index * ctx_count + ctx_index
    tokens_here = queries.shape[1]
    model_width = queries.shape[2]
    blocks_here = tokens_here // BLK
    score_scale = 1.0 / math.sqrt(HD)
    qheads = queries[0].reshape(tokens_here, H, HD)
    paired = jnp.concatenate([keys[0], values[0]], axis=-1)
    from_ctx = shifted(paired, "ctx", 1)
    from_grp = shifted_2(from_ctx, "grp", 1)
    previous = jnp.where(ctx_index == 0, from_grp, from_ctx)
    own_blocks = paired.reshape(blocks_here, BLK, 2 * model_width)
    prev_blocks = jnp.concatenate([previous[None], own_blocks[:-1]], axis=0)
    window = jnp.concatenate([prev_blocks, own_blocks], axis=1)
    near_keys = window[..., :model_width].reshape(blocks_here, 2 * BLK, H, HD)
    near_vals = window[..., model_width:].reshape(blocks_here, 2 * BLK, H, HD)
    block_ids = device_flat * blocks_here + jnp.arange(blocks_here, dtype=jnp.int32)
    near_scores = (
        jnp.einsum(
            "bqhd,bkhd->bhqk",
            qheads.reshape(blocks_here, BLK, H, HD),
            near_keys,
            preferred_element_type=jnp.float32,
        )
        * score_scale
    )
    window_index = jnp.arange(2 * BLK, dtype=jnp.int32)
    query_index = jnp.arange(BLK, dtype=jnp.int32)
    own_part = (window_index[None, :] >= BLK) & (
        window_index[None, :] - BLK <= query_index[:, None]
    )
    prev_part = (window_index[None, None, :] < BLK) & (block_ids >= 1)[:, None, None]
    near_mask = (own_part[None] | prev_part)[:, None]
    near_scores = jnp.where(near_mask, near_scores, masked_score)
    near_peak = near_scores.max(-1)
    near_weight = jnp.where(near_mask, jnp.exp(near_scores - near_peak[..., None]), 0.0)
    near_total = near_weight.sum(-1)
    near_summed = jnp.einsum(
        "bhqk,bkhd->bhqd",
        near_weight.astype(jnp.bfloat16),
        near_vals,
        preferred_element_type=jnp.float32,
    )
    running = (
        jnp.transpose(near_peak, (1, 0, 2)).reshape(H, tokens_here),
        jnp.transpose(near_total, (1, 0, 2)).reshape(H, tokens_here),
        jnp.transpose(near_summed, (1, 0, 2, 3)).reshape(H, tokens_here, HD),
    )
    qblock = device_flat * blocks_here + jnp.arange(tokens_here, dtype=jnp.int32) // BLK
    offsets = (jnp.arange(blocks_here, dtype=jnp.int32)[:, None] * BLK + summary_pos[0]).reshape(-1)
    local_summ = paired[offsets]
    summ_here = local_summ.shape[0]
    slot_block = jnp.arange(summ_here, dtype=jnp.int32) // SUMM
    per_group = gathered_copies(local_summ[None, None], "ctx", 1)
    shard_piece = lax.all_gather(per_group, "grp", axis=0, tiled=True)
    group_ids = jnp.arange(shard_piece.shape[0], dtype=jnp.int32)
    row_blocks = (
        (
            group_ids[:, None, None] * ctx_count
            + jnp.arange(ctx_count, dtype=jnp.int32)[None, :, None]
        )
        * blocks_here
        + slot_block[None, None, :]
    ).reshape(-1)
    running = fold_rows(
        running, qheads, qblock, shard_piece.reshape(-1, 2 * model_width), row_blocks, score_scale
    )
    result = running[2] / running[1][..., None]
    return (
        jnp.transpose(result, (1, 0, 2))
        .reshape(tokens_here, model_width)
        .astype(jnp.bfloat16)[None]
    )


def solution(mesh):
    placed = (
        P("grp", "ctx", None),
        P("grp", "ctx", None),
        P("grp", "ctx", None),
        P("grp", "ctx", None),
    )
    return jax.shard_map(
        shards, mesh=mesh, in_specs=placed, out_specs=P("grp", "ctx", None), check_vma=False
    )
```

profile of v0, /device:TPU:1, one launch (start us, length us, event | category | flops | bytes accessed | tf_op | source)
XLA Modules:
  0.0 235.4 jit_solution(3036755224656347395)
XLA Ops:
  7.2 1.4 fusion.33
  9.3 47.6 %all_to_all.5 = bf16[32,1,1,8,1024]{4,3,2,1,0:T(8,128)(2,1)} all-to-all(bf16[32,1,1,8,1024]{4,3,2,1,0:T(8,128)(2,1)S(1)} %broadcast_in_dim.76), channel_id=1, replica_groups=mesh['ctx'=32,'grp'=16] {'ctx'}, dimensions={0} | all-to-all | bytes 1048576 | tf_op jit(solution)/shard_map/all_to_all | solution.py:31
  56.9 3.4 %collective-permute-start = (bf16[512,1024]{1,0:T(8,128)(2,1)S(1)}, bf16[512,1024]{1,0:T(8,128)(2,1)}, u32[]{:S(2)}, u32[]{:S(2)}) collective-permute-start(bf16[512,1024]{1,0:T(8,128)(2,1)S(1)} %get-tuple-element.169), channel_id=1, source_target_pairs={{0,16},{16,32},{32,48},{48,64},{64,80},{80,96},{96,112},{112,128},... | collective-permute-start | bytes 3145736 | tf_op jit(solution)/shard_map/ppermute | solution.py:20
  60.3 23.9 %collective-permute-done = bf16[512,1024]{1,0:T(8,128)(2,1)} collective-permute-done((bf16[512,1024]{1,0:T(8,128)(2,1)S(1)}, bf16[512,1024]{1,0:T(8,128)(2,1)}, u32[]{:S(2)}, u32[]{:S(2)}) %collective-permute-start) | collective-permute-done | bytes 1048608 | tf_op jit(solution)/shard_map/ppermute | solution.py:20
  84.3 5.4 %collective-permute-start.1 = (bf16[512,1024]{1,0:T(8,128)(2,1)}, bf16[512,1024]{1,0:T(8,128)(2,1)S(1)}, u32[]{:S(2)}, u32[]{:S(2)}) collective-permute-start(bf16[512,1024]{1,0:T(8,128)(2,1)} %collective-permute-done), channel_id=1, source_target_pairs={{0,1},{1,2},{2,3},{3,4},{4,5},{5,6},{6,7},{7,8},{8,9},{9,10},{10,1... | collective-permute-start | bytes 3145736 | tf_op jit(solution)/shard_map/ppermute | solution.py:26
  89.7 1.3 copy.20
  92.3 17.1 %collective-permute-done.1 = bf16[512,1024]{1,0:T(8,128)(2,1)S(1)} collective-permute-done((bf16[512,1024]{1,0:T(8,128)(2,1)}, bf16[512,1024]{1,0:T(8,128)(2,1)S(1)}, u32[]{:S(2)}, u32[]{:S(2)}) %collective-permute-start.1) | collective-permute-done | bytes 1048608 | tf_op jit(solution)/shard_map/ppermute | solution.py:26
  109.5 1.2 pad_maximum_fusion
  110.8 1.5 copy.19
  112.2 1.4 copy.21
  113.6 2.8 %fusion.19 = (f32[8,512]{1,0:T(8,128)S(1)}, f32[8,1024,512]{2,1,0:T(8,128)S(1)}) fusion(pred[512,1024]{0,1:T(8,128)(4,1)S(1)} %fusion.26, bf16[1024,8,64]{0,2,1:T(8,128)(2,1)S(1)} %bitcast.76, bf16[512,8,64]{0,2,1:T(8,128)(2,1)S(1)} %bitcast.73), kind=kOutput, calls=%fused_computation.29 | convolution fusion | flops 549449728 | bytes 18890752 | tf_op jit(solution)/shard_map/bqhd,bkhd->bhqk/dot_general | solution.py:103
  116.4 5.0 %fusion.22 = f32[8,512,64]{1,2,0:T(8,128)} fusion(bf16[1024,8,64]{0,2,1:T(8,128)(2,1)S(1)} %bitcast.79, f32[8,1024,512]{2,1,0:T(8,128)S(1)} %get-tuple-element.171, f32[8,512]{1,0:T(8,128)S(1)} %get-tuple-element.236, pred[512,1024]{0,1:T(8,128)(4,1)S(1)} %fusion.26), kind=kOutput, calls=%fused_computation.32 | convolution fusion | flops 557842432 | bytes 19415040 | tf_op jit(solution)/shard_map/bhqk,bkhd->bhqd/dot_general | solution.py:122
  121.4 4.0 %fusion.21 = f32[8,512]{1,0:T(8,128)S(1)} fusion(f32[8,1024,512]{2,1,0:T(8,128)S(1)} %get-tuple-element.171, f32[8,512]{1,0:T(8,128)S(1)} %get-tuple-element.236, pred[512,1024]{0,1:T(8,128)(4,1)S(1)} %fusion.26), kind=kLoop, calls=%fused_computation.31 | loop fusion | flops 20967424 | bytes 17334272 | tf_op jit(solution)/shard_map/reduce_sum | solution.py:121
  125.5 17.6 %all-gather.3.cloned.1.call-done = bf16[512,1,1,8,1024]{4,3,2,1,0:T(8,128)(2,1)} async-done(((bf16[32,1,1,8,1024]{4,3,2,1,0:T(8,128)(2,1)}), bf16[512,1,1,8,1024]{4,3,2,1,0:T(8,128)(2,1)}) %all-gather.3.cloned.1.call-update) | async-done | bytes 8388624 | tf_op jit(solution)/shard_map/all_gather | solution.py:139
  143.1 83.1 %while.17 = (s32[]{:T(128)}, f32[8,512]{1,0:T(8,128)S(1)}, f32[8,512]{1,0:T(8,128)S(1)}, f32[8,512,64]{1,2,0:T(8,128)}, s32[8,512]{1,0:T(8,128)S(1)}, /*index=5*...) while((s32[]{:T(128)}, f32[8,512]{1,0:T(8,128)S(1)}, ...), condition=%wide.region_5.6_spmd.clone, body=%wide.region_2.5_spmd.clone.sunk | while | flops 564933632 | bytes 36448360 | solution.py:78
  143.3 1.3 constant_dynamic-slice_fusion.5
  145.3 1.5 fusion.56
  146.8 2.0 fusion.57
  148.8 4.6 %fusion.58 = f32[8,512,64]{1,2,0:T(8,128)} fusion(bf16[512,8,64]{0,2,1:T(8,128)(2,1)S(1)} %bitcast.75, f32[8,512,512]{2,1,0:T(8,128)S(1)} %get-tuple-element.231, f32[8,512]{1,0:T(8,128)S(1)} %max.8, pred[512,512]{0,1:T(8,128)(4,1)S(1)} %broadcast_compare_fusion.2, f32[8,512,64]{1,2,0:T(8,128)} %get-tuple-element.247, ...), kind=kOutput, calls=%fused_computation.9.clone.1 | convolution fusion | flops 279445504 | bytes 11304960 | tf_op jit(solution)/shard_map/while/body/eval_jaxpr/hqr,rhd->hqd/dot_general | solution.py:65
  153.7 1.3 constant_dynamic-slice_fusion.5
  155.7 1.5 fusion.56
  157.2 2.0 fusion.57
  159.2 4.6 %fusion.58 = f32[8,512,64]{1,2,0:T(8,128)} fusion(bf16[512,8,64]{0,2,1:T(8,128)(2,1)S(1)} %bitcast.75, f32[8,512,512]{2,1,0:T(8,128)S(1)} %get-tuple-element.231, f32[8,512]{1,0:T(8,128)S(1)} %max.8, pred[512,512]{0,1:T(8,128)(4,1)S(1)} %broadcast_compare_fusion.2, f32[8,512,64]{1,2,0:T(8,128)} %get-tuple-element.247, ...), kind=kOutput, calls=%fused_computation.9.clone.1 | convolution fusion | flops 279445504 | bytes 11304960 | tf_op jit(solution)/shard_map/while/body/eval_jaxpr/hqr,rhd->hqd/dot_general | solution.py:65
  164.1 1.3 constant_dynamic-slice_fusion.5
  166.1 1.5 fusion.56
  167.6 2.0 fusion.57
  169.6 4.6 %fusion.58 = f32[8,512,64]{1,2,0:T(8,128)} fusion(bf16[512,8,64]{0,2,1:T(8,128)(2,1)S(1)} %bitcast.75, f32[8,512,512]{2,1,0:T(8,128)S(1)} %get-tuple-element.231, f32[8,512]{1,0:T(8,128)S(1)} %max.8, pred[512,512]{0,1:T(8,128)(4,1)S(1)} %broadcast_compare_fusion.2, f32[8,512,64]{1,2,0:T(8,128)} %get-tuple-element.247, ...), kind=kOutput, calls=%fused_computation.9.clone.1 | convolution fusion | flops 279445504 | bytes 11304960 | tf_op jit(solution)/shard_map/while/body/eval_jaxpr/hqr,rhd->hqd/dot_general | solution.py:65
  174.5 1.3 constant_dynamic-slice_fusion.5
  176.4 1.5 fusion.56
  177.9 2.0 fusion.57
  180.0 4.6 %fusion.58 = f32[8,512,64]{1,2,0:T(8,128)} fusion(bf16[512,8,64]{0,2,1:T(8,128)(2,1)S(1)} %bitcast.75, f32[8,512,512]{2,1,0:T(8,128)S(1)} %get-tuple-element.231, f32[8,512]{1,0:T(8,128)S(1)} %max.8, pred[512,512]{0,1:T(8,128)(4,1)S(1)} %broadcast_compare_fusion.2, f32[8,512,64]{1,2,0:T(8,128)} %get-tuple-element.247, ...), kind=kOutput, calls=%fused_computation.9.clone.1 | convolution fusion | flops 279445504 | bytes 11304960 | tf_op jit(solution)/shard_map/while/body/eval_jaxpr/hqr,rhd->hqd/dot_general | solution.py:65
  184.9 1.3 constant_dynamic-slice_fusion.5
  186.8 1.5 fusion.56
  188.3 2.0 fusion.57
  190.4 4.6 %fusion.58 = f32[8,512,64]{1,2,0:T(8,128)} fusion(bf16[512,8,64]{0,2,1:T(8,128)(2,1)S(1)} %bitcast.75, f32[8,512,512]{2,1,0:T(8,128)S(1)} %get-tuple-element.231, f32[8,512]{1,0:T(8,128)S(1)} %max.8, pred[512,512]{0,1:T(8,128)(4,1)S(1)} %broadcast_compare_fusion.2, f32[8,512,64]{1,2,0:T(8,128)} %get-tuple-element.247, ...), kind=kOutput, calls=%fused_computation.9.clone.1 | convolution fusion | flops 279445504 | bytes 11304960 | tf_op jit(solution)/shard_map/while/body/eval_jaxpr/hqr,rhd->hqd/dot_general | solution.py:65
  195.3 1.3 constant_dynamic-slice_fusion.5
  197.2 1.5 fusion.56
  198.7 2.0 fusion.57
  200.8 4.6 %fusion.58 = f32[8,512,64]{1,2,0:T(8,128)} fusion(bf16[512,8,64]{0,2,1:T(8,128)(2,1)S(1)} %bitcast.75, f32[8,512,512]{2,1,0:T(8,128)S(1)} %get-tuple-element.231, f32[8,512]{1,0:T(8,128)S(1)} %max.8, pred[512,512]{0,1:T(8,128)(4,1)S(1)} %broadcast_compare_fusion.2, f32[8,512,64]{1,2,0:T(8,128)} %get-tuple-element.247, ...), kind=kOutput, calls=%fused_computation.9.clone.1 | convolution fusion | flops 279445504 | bytes 11304960 | tf_op jit(solution)/shard_map/while/body/eval_jaxpr/hqr,rhd->hqd/dot_general | solution.py:65
  205.7 1.3 constant_dynamic-slice_fusion.5
  207.6 1.5 fusion.56
  209.1 2.0 fusion.57
  211.2 4.6 %fusion.58 = f32[8,512,64]{1,2,0:T(8,128)} fusion(bf16[512,8,64]{0,2,1:T(8,128)(2,1)S(1)} %bitcast.75, f32[8,512,512]{2,1,0:T(8,128)S(1)} %get-tuple-element.231, f32[8,512]{1,0:T(8,128)S(1)} %max.8, pred[512,512]{0,1:T(8,128)(4,1)S(1)} %broadcast_compare_fusion.2, f32[8,512,64]{1,2,0:T(8,128)} %get-tuple-element.247, ...), kind=kOutput, calls=%fused_computation.9.clone.1 | convolution fusion | flops 279445504 | bytes 11304960 | tf_op jit(solution)/shard_map/while/body/eval_jaxpr/hqr,rhd->hqd/dot_general | solution.py:65
  216.1 1.3 constant_dynamic-slice_fusion.5
  218.0 1.5 fusion.56
  219.5 2.0 fusion.57
  221.6 4.6 %fusion.58 = f32[8,512,64]{1,2,0:T(8,128)} fusion(bf16[512,8,64]{0,2,1:T(8,128)(2,1)S(1)} %bitcast.75, f32[8,512,512]{2,1,0:T(8,128)S(1)} %get-tuple-element.231, f32[8,512]{1,0:T(8,128)S(1)} %max.8, pred[512,512]{0,1:T(8,128)(4,1)S(1)} %broadcast_compare_fusion.2, f32[8,512,64]{1,2,0:T(8,128)} %get-tuple-element.247, ...), kind=kOutput, calls=%fused_computation.9.clone.1 | convolution fusion | flops 279445504 | bytes 11304960 | tf_op jit(solution)/shard_map/while/body/eval_jaxpr/hqr,rhd->hqd/dot_general | solution.py:65
  226.2 1.3 divide_convert_fusion
  (82 shorter events, 10.6 us)
Async XLA Ops:
  6.5 136.6 %all-gather.3.cloned.1.call-start = ((), (), s32[]{:S(2)}) async-start(), calls=%async_computation.1 | async-start | bytes 8912896 | tf_op jit(solution)/shard_map/all_gather | solution.py:139
  56.9 27.4 %collective-permute-start = (bf16[512,1024]{1,0:T(8,128)(2,1)S(1)}, bf16[512,1024]{1,0:T(8,128)(2,1)}, u32[]{:S(2)}, u32[]{:S(2)}) collective-permute-start(bf16[512,1024]{1,0:T(8,128)(2,1)S(1)} %get-tuple-element.169), channel_id=1, source_target_pairs={{0,16},{16,32},{32,48},{48,64},{64,80},{80,96},{96,112},{112,128},... | collective-permute-start | bytes 3145736 | tf_op jit(solution)/shard_map/ppermute | solution.py:20
  84.3 25.1 %collective-permute-start.1 = (bf16[512,1024]{1,0:T(8,128)(2,1)}, bf16[512,1024]{1,0:T(8,128)(2,1)S(1)}, u32[]{:S(2)}, u32[]{:S(2)}) collective-permute-start(bf16[512,1024]{1,0:T(8,128)(2,1)} %collective-permute-done), channel_id=1, source_target_pairs={{0,1},{1,2},{2,3},{3,4},{4,5},{5,6},{6,7},{7,8},{8,9},{9,10},{10,1... | collective-permute-start | bytes 3145736 | tf_op jit(solution)/shard_map/ppermute | solution.py:26
  113.6 2.8 %copy-start = (bf16[1,1024,512]{1,2,0:T(8,128)(2,1)S(1)}, bf16[1,1024,512]{1,2,0:T(8,128)(2,1)}, u32[]{:S(2)}) copy-start(bf16[1,1024,512]{1,2,0:T(8,128)(2,1)} %copy.21) | copy-start | bytes 3145732
Sparse Core Ops, SparseCore 0:
  57.0 86.0 all-gather.2
where the time goes:
time: 236 us; the launch traced here: 235 us
  waiting for transfers between devices  58.7 us (25%)
  matrix products  56.9 us (24%)
  blocking collectives  47.6 us (20%)
  other arithmetic  28.1 us (12%)
  local copies, waits for them, and re-layouts  21.3 us (9%)
  between operations  13.5 us (6%)
  starting transfers between devices  8.83 us (4%)
    all_to_all x1, blocking collectives, copy_for_each(): return lax.all_to_all(copies, axis, split_axis=0, concat_axis=0, tiled=True)  47.6 us
    dot_general x8, matrix products, update(): jnp.einsum('hqr,rhd->hqd', weights.astype(jnp.bfloat16), tile_vals, prefe...  37.2 us
    ppermute x1, waiting for transfers between devices, shifted(): return lax.ppermute(value, axis, pairs)  23.9 us
    all_gather x1, waiting for transfers between devices, shards(): shard_piece = lax.all_gather(per_group, 'grp', axis=0, tiled=True)  17.6 us
    ppermute x1, waiting for transfers between devices, shifted_2(): return lax.ppermute(value, axis, pairs)  17.1 us
    reduce_sum x8, other arithmetic, update(): total_new = total_old * rescale + weights.sum(-1)  16.2 us
    dynamic_slice x24, local copies, waits for them, and re-layouts, fold_rows(): result, unused = lax.scan(update, running, tile_list)  14.8 us
    dot_general x8, matrix products, update(): jnp.einsum('qhd,rhd->hqr', qheads, tile_keys, preferred_element_type=jnp....  11.9 us
  transfers between devices with their start and end apart: 3, of which 3 were waited for; matrix products, arithmetic and copies ran while one was open for 8% of the time, Pallas kernels for 0%

commit v1 on v0

v1 whole, which is shorter than its diff:
```python
import functools
import math

import jax
import jax.numpy as jnp
from jax import lax
from jax.experimental import pallas as pl
from jax.experimental.pallas import tpu as pltpu
from jax.sharding import PartitionSpec as P

H = 8
HD = 64
BLK = 512
SUMM = 8
HALF = 256
ACC = 80
SEND = 72
RATE = math.log2(math.e) / math.sqrt(HD)
FLOOR = -1e29
NONE = -1e30
bf16 = jnp.bfloat16
f32 = jnp.float32


def dot(a, b):
    return lax.dot_general(a, b, (((1,), (0,)), ((), ())), preferred_element_type=f32)


def fold(parts, values_t, peak, acc):
    top = peak
    for part in parts:
        top = jnp.maximum(top, part.max(0, keepdims=True))
    weights = [jnp.exp2((part - top) * RATE).astype(bf16) for part in parts]
    rescale = jnp.exp2((peak - top) * RATE)
    acc = acc * rescale + dot(values_t, jnp.concatenate(weights, axis=0))
    return top, acc


def prep_kernel(pos_ref, q_ref, k_ref, v_ref, send_ref, kv_ref):
    kv_ref[:, : H * HD] = k_ref[...]
    kv_ref[:, H * HD :] = v_ref[...]
    slot = lax.broadcasted_iota(jnp.int32, (16, BLK), 0)
    token = lax.broadcasted_iota(jnp.int32, (16, BLK), 1)
    wanted = jnp.full((16, BLK), -1, jnp.int32)
    for j in range(SUMM):
        wanted = jnp.where(slot == j, pos_ref[j], wanted)
    pick = jnp.where(token == wanted, 1.0, 0.0).astype(bf16)
    k_rows = dot(pick, k_ref[...])[:SUMM]
    v_rows = dot(pick, v_ref[...])[:SUMM]
    blank = jnp.zeros((SUMM, HALF - 128), f32)
    q_t = q_ref[...].T
    for h in range(H):
        part = slice(h * HD, (h + 1) * HD)
        rows = jnp.concatenate([v_rows[:, part], k_rows[:, part], blank], axis=1).astype(bf16)
        for half in range(2):
            send_ref[2 * h + half, :HD] = q_t[part, half * HALF : (half + 1) * HALF]
            send_ref[2 * h + half, HD:] = rows


def spread_kernel(where_ref, got_ref, out_ref):
    odd = where_ref[1] > 0
    pieces = [jnp.where(odd, got_ref[2 * i + 1], got_ref[2 * i]) for i in range(8)]
    rows = jnp.concatenate(pieces, axis=0)
    for z in range(out_ref.shape[0]):
        out_ref[z] = rows


def near_kernel(own, has_ref, qt_ref, *rest):
    if own:
        k_ref, v_ref, acc_ref, peak_ref, vt_ref = rest
        v_t = v_ref[...].T
    else:
        k_ref, acc_in, peak_in, acc_ref, peak_ref, vt_ref = rest
        v_t = k_ref[:, H * HD :].T
    for h in range(H):
        vt_ref[h, :HD] = v_t[h * HD : (h + 1) * HD]
        vt_ref[h, HD:] = jnp.ones((ACC - HD, BLK), bf16)
    zeros = jnp.zeros((HD, HALF), bf16)
    key_at = lax.broadcasted_iota(jnp.int32, (HALF, HALF), 0)
    query_at = lax.broadcasted_iota(jnp.int32, (HALF, HALF), 1)
    causal = key_at <= query_at
    for h in range(H):
        pair = slice((h // 2) * 128, (h // 2 + 1) * 128)
        for half in range(2):
            cols = slice(half * HALF, (half + 1) * HALF)
            q_t = qt_ref[2 * h + half, :HD]
            q_t = jnp.concatenate([q_t, zeros] if h % 2 == 0 else [zeros, q_t], axis=0)
            if own:
                count = (half + 1) * HALF
                parts = [dot(k_ref[i : i + HALF, pair], q_t) for i in range(0, count, HALF)]
                parts[-1] = jnp.where(causal, parts[-1], NONE)
                peak = jnp.full((1, HALF), FLOOR, f32)
                acc = jnp.zeros((ACC, HALF), f32)
            else:
                count = BLK
                parts = [dot(k_ref[i : i + HALF, pair], q_t) for i in range(0, count, HALF)]
                peak = peak_in[h, :1, cols]
                acc = acc_in[h, :, cols]
            new_peak, new_acc = fold(parts, vt_ref[h, :, :count], peak, acc)
            if not own:
                has = has_ref[0] > 0
                new_peak = jnp.where(has, new_peak, peak)
                new_acc = jnp.where(has, new_acc, acc)
            acc_ref[h, :, cols] = new_acc
            peak_ref[h, :, cols] = jnp.broadcast_to(new_peak, (8, HALF))


def far_kernel(where_ref, q_ref, s00_ref, s01_ref, s10_ref, s11_ref, out_ref, vt_ref, k_ref, qt_ref, even_ref, odd_ref):
    c = where_ref[0]
    half = where_ref[1]
    y = c // 16
    sets = (s00_ref, s01_ref, s10_ref, s11_ref)
    part = 256
    tile = 4 * part
    wide = 2 * HALF
    lane = lax.broadcasted_iota(jnp.int32, (part, 128), 1)
    row = lax.broadcasted_iota(jnp.int32, (part, 128), 0)
    age = 64 * ((row % 16) // SUMM) + row // 16 - 32 * lane
    age = jnp.where(lane < 16, age, -(1 << 20))
    key_lane = lane >= HD
    for p in range(4):
        for i, ref in enumerate(sets):
            rows = ref[:, p * 16 : p * 16 + 16].reshape(part, 128)
            start = 128 * p + 32 * (half ^ (i % 2)) + 16 * (y ^ (i // 2))
            bias = jnp.where(age <= c - 2 - start, 0.0, NONE).astype(bf16)
            k_ref[p, i * part : (i + 1) * part] = jnp.where(key_lane, rows, bias)
            vt_ref[p, :, i * part : (i + 1) * part] = rows.T[:ACC]
        vt_ref[p, HD:] = jnp.ones((ACC - HD, tile), bf16)
    at = lax.broadcasted_iota(jnp.int32, (HD, HALF), 0)
    for g in range(16):
        one_hot = jnp.where(at == g, 1.0, 0.0).astype(bf16)
        cols = slice((g % 2) * HALF, (g % 2 + 1) * HALF)
        qt_ref[g // 2, :, cols] = jnp.concatenate([one_hot, q_ref[g, :HD]], axis=0)

    def scores(pair, p, buf, peak):
        for i in range(4):
            piece = dot(k_ref[p, i * part : (i + 1) * part], qt_ref[pair])
            buf[p, i * part : (i + 1) * part] = piece
            peak = jnp.maximum(peak, piece.reshape(part // 8, 8, wide).max(0))
        return peak

    def values(p, buf, top, acc):
        weights = [
            jnp.exp2((buf[p, i * part : (i + 1) * part] - top) * RATE).astype(bf16)
            for i in range(4)
        ]
        return acc + dot(vt_ref[p], jnp.concatenate(weights, axis=0))

    def finish(pair, top, acc):
        total = acc[HD : HD + 1]
        some = total > 0.0
        safe = jnp.where(some, total, 1.0)
        result = (acc[:HD] * (1.0 / safe)).astype(bf16)
        level = jnp.where(some, top * RATE + jnp.log2(safe), NONE)
        high = level.astype(bf16)
        rest = level - high.astype(f32)
        mid = rest.astype(bf16)
        low = (rest - mid.astype(f32)).astype(bf16)
        stats = jnp.concatenate([high, mid, low, jnp.zeros((SEND - HD - 3, wide), bf16)], axis=0)
        for j in range(2):
            cols = slice(j * HALF, (j + 1) * HALF)
            out_ref[2 * pair + j, :HD] = result[:, cols]
            out_ref[2 * pair + j, HD:] = stats[:, cols]

    floor = jnp.full((8, wide), FLOOR, f32)
    empty = jnp.zeros((ACC, wide), f32)

    def turn(pair, count, more, this, other, peak):
        top = peak.max(0, keepdims=True)
        later = jnp.minimum(pair + 1, 7)

        def both(p, carry):
            acc, ahead = carry
            ahead = scores(later, p, other, ahead)
            acc = values(p, this, top, acc)
            return acc, ahead

        acc, ahead = lax.fori_loop(0, count, both, (empty, floor))
        if more:
            ahead = scores(later, jnp.minimum(count, 3), other, ahead)
        finish(pair, top, acc)
        return ahead

    def quad(i, peak):
        peak = turn(2 * i, i + 1, False, even_ref, odd_ref, peak)
        return turn(2 * i + 1, i + 1, True, odd_ref, even_ref, peak)

    lax.fori_loop(0, 4, quad, scores(0, 0, even_ref, floor))


def merge_kernel(acc_ref, peak_ref, far_ref, out_ref):
    for h in range(H):
        columns = []
        for half in range(2):
            cols = slice(half * HALF, (half + 1) * HALF)
            far = far_ref[2 * h + half]
            stats = far[HD:].astype(f32)
            level = stats[0:1] + (stats[1:2] + stats[2:3])
            near = peak_ref[h, :1, cols] * RATE
            top = jnp.maximum(near, level)
            near = jnp.exp2(near - top)
            level = jnp.exp2(level - top)
            total = acc_ref[h, HD : HD + 1, cols] * near + level
            result = acc_ref[h, :HD, cols] * (near / total) + far[:HD].astype(f32) * (level / total)
            columns.append(result)
        wide = jnp.concatenate(columns, axis=1).astype(bf16)
        if h % 2 == 0:
            first = wide
        else:
            both = jnp.concatenate([first, wide], axis=0)
            out_ref[:, (h // 2) * 128 : (h // 2 + 1) * 128] = both.T


def vmem(count):
    return [pl.BlockSpec(memory_space=pltpu.VMEM)] * count


SMEM = pl.BlockSpec(memory_space=pltpu.SMEM)


LIMIT = pltpu.CompilerParams(vmem_limit_bytes=24 << 20)


def cost(flops, size, exps=0):
    return pl.CostEstimate(flops=flops, bytes_accessed=size, transcendentals=exps)


def near(own, has, *args):
    shapes = (
        jax.ShapeDtypeStruct((H, ACC, BLK), f32),
        jax.ShapeDtypeStruct((H, 8, BLK), f32),
    )
    return pl.pallas_call(
        functools.partial(near_kernel, own),
        out_shape=shapes,
        in_specs=[SMEM] + vmem(len(args)),
        out_specs=tuple(vmem(2)),
        scratch_shapes=[pltpu.VMEM((H, ACC, BLK), bf16)],
        compiler_params=LIMIT,
        cost_estimate=cost(2 * H * BLK * BLK * 256, 4 << 20, H * BLK * BLK),
        name="near_own" if own else "near_prev",
    )(has, *args)


def shards(queries, keys, values, summary_pos):
    c = lax.axis_index("ctx")
    g = lax.axis_index("grp")
    groups, per_group = lax.axis_size("grp"), lax.axis_size("ctx")
    layers = per_group // 2
    same_y = [[y * layers + z for z in range(layers)] for y in range(2)]
    other_y = [(i, (i + layers) % per_group) for i in range(per_group)]
    other_core = [(i, i ^ 1) for i in range(groups)]
    q, k, v = queries[0], keys[0], values[0]

    where = jnp.stack([c, g % 2]).astype(jnp.int32)
    has = jnp.where(c + g > 0, 1, 0).astype(jnp.int32)[None]
    send, kv = pl.pallas_call(
        prep_kernel,
        out_shape=(
            jax.ShapeDtypeStruct((groups, SEND, HALF), bf16),
            jax.ShapeDtypeStruct((BLK, 2 * H * HD), bf16),
        ),
        in_specs=[SMEM] + vmem(3),
        out_specs=tuple(vmem(2)),
        cost_estimate=cost(4 * 16 * BLK * BLK, 3 << 20),
        name="prep",
    )(summary_pos[0, 0], q, k, v)
    carried = near(True, has, send, k, v)

    got = lax.all_to_all(send, "grp", 0, 0, tiled=True)
    mine = pl.pallas_call(
        spread_kernel,
        out_shape=jax.ShapeDtypeStruct((layers, 64, 128), bf16),
        grid=(1,),
        in_specs=[SMEM, pl.BlockSpec((groups, SUMM, 128), lambda i: (0, HD // SUMM, 0))],
        out_specs=pl.BlockSpec((layers, 64, 128), lambda i: (0, 0, 0)),
        compiler_params=LIMIT,
        name="spread",
    )(where, got)
    s00 = lax.all_to_all(mine, "ctx", 0, 0, tiled=True, axis_index_groups=same_y)
    s10 = lax.ppermute(s00, "ctx", other_y)
    s01 = lax.ppermute(s00, "grp", other_core)
    s11 = lax.ppermute(s10, "grp", other_core)

    kv, unused = lax.optimization_barrier((kv, s00))
    flat = [t * groups + s for s in range(groups) for t in range(per_group)]
    kv_prev = lax.ppermute(kv, ("ctx", "grp"), list(zip(flat[:-1], flat[1:])))

    partial = pl.pallas_call(
        far_kernel,
        out_shape=jax.ShapeDtypeStruct((groups, SEND, HALF), bf16),
        in_specs=[SMEM] + vmem(5),
        out_specs=vmem(1)[0],
        scratch_shapes=[
            pltpu.VMEM((4, ACC, 1024), bf16),
            pltpu.VMEM((4, 1024, 128), bf16),
            pltpu.VMEM((groups // 2, 128, 2 * HALF), bf16),
            pltpu.VMEM((4, 1024, 2 * HALF), f32),
            pltpu.VMEM((4, 1024, 2 * HALF), f32),
        ],
        compiler_params=pltpu.CompilerParams(vmem_limit_bytes=32 << 20),
        cost_estimate=cost(2 * 40 * 1024 * HALF * 256, 3 << 20, 40 * 1024 * HALF),
        name="far",
    )(where, got, s00, s01, s10, s11)
    far = lax.all_to_all(partial, "grp", 0, 0, tiled=True)
    acc, peak = near(False, has, send, kv_prev, *carried)

    out = pl.pallas_call(
        merge_kernel,
        out_shape=jax.ShapeDtypeStruct((BLK, H * HD), bf16),
        in_specs=vmem(3),
        out_specs=vmem(1)[0],
        compiler_params=LIMIT,
        cost_estimate=cost(H * BLK * HD * 8, 3 << 20),
        name="merge",
    )(acc, peak, far)
    return out[None]


def solution(mesh):
    placed = P("grp", "ctx", None)
    return jax.shard_map(
        shards, mesh=mesh, in_specs=(placed,) * 4, out_specs=placed, check_vma=False
    )
```

time: 236 us -> 108 us (0.46)
  the two profiles are of different devices: /device:TPU:1 before, /device:TPU:10 now
where the time goes in v1:
time: 108 us
  blocking collectives  33.1 us (31%)
  Pallas kernels  30 us (28%)
  starting transfers between devices  23.3 us (22%)
  waiting for transfers between devices  19.1 us (18%)
  local copies, waits for them, and re-layouts  2.22 us (2%)
    all_to_all x1, blocking collectives, shards(): lax.all_to_all(mine, 'ctx', 0, 0, tiled=True, axis_index_groups=same_y)  33.1 us
    pallas_call x1, Pallas kernels, shards(): pl.pallas_call(far_kernel, out_shape=jax.ShapeDtypeStruct((groups, SEND,...  17 us
    all_to_all x1, waiting for transfers between devices, shards(): got = lax.all_to_all(send, 'grp', 0, 0, tiled=True)  9.02 us
    pallas_call x2, Pallas kernels, near(): pl.pallas_call(functools.partial(near_kernel, own), out_shape=shapes, in_...  8.36 us
    all_to_all x1, starting transfers between devices, shards(): got = lax.all_to_all(send, 'grp', 0, 0, tiled=True)  6.58 us
    ppermute x1, waiting for transfers between devices, shards(): s10 = lax.ppermute(s00, 'ctx', other_y)  5.17 us
    all_to_all x1, starting transfers between devices, shards(): far = lax.all_to_all(partial, 'grp', 0, 0, tiled=True)  4.95 us
    ppermute x1, waiting for transfers between devices, shards(): kv_prev = lax.ppermute(kv, ('ctx', 'grp'), list(zip(flat[:-1], flat[1:])))  4.93 us
  transfers between devices with their start and end apart: 6, of which 3 were waited for; matrix products, arithmetic and copies ran while one was open for 0% of the time, Pallas kernels for 23%

profile of v1, /device:TPU:10, one launch (start us, length us, event | category | flops | bytes accessed | tf_op | source)
XLA Modules:
  0.0 108.0 jit_solution(16006344630708250776)
XLA Ops:
  0.0 2.9 %prep.1 = (bf16[16,72,256]{2,1,0:T(8,128)(2,1)}, bf16[512,1024]{1,0:T(8,128)(2,1)}) custom-call(s32[8]{0:T(128)} %bitcast.13, bf16[512,512]{1,0:T(8,128)(2,1)} %bitcast.12, bf16[512,512]{1,0:T(8,128)(2,1)} %bitcast.8, bf16[512,512]{1,0:T(8,128)(2,1)} %bitcast.10), custom_call_target="tpu_custom_call" | custom-call | flops 16777216 | bytes 3145728 | tf_op jit(solution)/shard_map/prep/pallas_call | solution.py:257
  2.9 6.6 %all-to-all-start = ((bf16[16,72,256]{2,1,0:T(8,128)(2,1)}), bf16[16,72,256]{2,1,0:T(8,128)(2,1)S(1)}, u32[]{:S(2)}, u32[]{:S(2)}) async-start(bf16[16,72,256]{2,1,0:T(8,128)(2,1)} %get-tuple-element.12.qt_ref), calls=%async_computation | async-start | bytes 1179648 | tf_op jit(solution)/shard_map/all_to_all | solution.py:270
  9.5 0.1 pad_add_fusion.where_ref
  9.6 9.0 %all-to-all-done.got_ref.q_ref = bf16[16,72,256]{2,1,0:T(8,128)(2,1)S(1)} async-done(((bf16[16,72,256]{2,1,0:T(8,128)(2,1)}), bf16[16,72,256]{2,1,0:T(8,128)(2,1)S(1)}, u32[]{:S(2)}, u32[]{:S(2)}) %all-to-all-start) | async-done | bytes 589856 | tf_op jit(solution)/shard_map/all_to_all | solution.py:270
  18.6 0.6 spread.1
  19.2 33.1 %all_to_all.15.s00_ref = bf16[16,64,128]{2,1,0:T(8,128)(2,1)S(1)} all-to-all(bf16[16,64,128]{2,1,0:T(8,128)(2,1)S(1)} %spread.1), channel_id=1, replica_groups={{0,16,32,48,64,80,96,112,128,144,160,176,192,208,224,240},{256,272,288,..., dimensions={0} | all-to-all | bytes 524288 | tf_op jit(solution)/shard_map/all_to_all | solution.py:280
  52.3 3.2 %collective-permute-start.2 = (bf16[16,64,128]{2,1,0:T(8,128)(2,1)S(1)}, bf16[16,64,128]{2,1,0:T(8,128)(2,1)S(1)}, u32[]{:S(2)}, u32[]{:S(2)}) collective-permute-start(bf16[16,64,128]{2,1,0:T(8,128)(2,1)S(1)} %all_to_all.15.s00_ref), channel_id=1, source_target_pairs={{0,256},{16,272},{32,288},{48,304},{64,320},{80,336},{96,352},{112... | collective-permute-start | bytes 786440 | tf_op jit(solution)/shard_map/ppermute | solution.py:281
  55.6 1.9 %collective-permute-start.1 = (bf16[16,64,128]{2,1,0:T(8,128)(2,1)S(1)}, bf16[16,64,128]{2,1,0:T(8,128)(2,1)S(1)}, u32[]{:S(2)}, u32[]{:S(2)}) collective-permute-start(bf16[16,64,128]{2,1,0:T(8,128)(2,1)S(1)} %all_to_all.15.s00_ref), channel_id=1, source_target_pairs={{0,1},{1,0},{2,3},{3,2},{4,5},{5,4},{6,7},{7,6},{8,9},{9,8},{10,11... | collective-permute-start | bytes 786440 | tf_op jit(solution)/shard_map/ppermute | solution.py:282
  57.5 5.2 %collective-permute-done.2.s10_ref = bf16[16,64,128]{2,1,0:T(8,128)(2,1)S(1)} collective-permute-done((bf16[16,64,128]{2,1,0:T(8,128)(2,1)S(1)}, bf16[16,64,128]{2,1,0:T(8,128)(2,1)S(1)}, u32[]{:S(2)}, u32[]{:S(2)}) %collective-permute-start.2) | collective-permute-done | bytes 262176 | tf_op jit(solution)/shard_map/ppermute | solution.py:281
  62.7 1.9 %collective-permute-start.3 = (bf16[16,64,128]{2,1,0:T(8,128)(2,1)S(1)}, bf16[16,64,128]{2,1,0:T(8,128)(2,1)S(1)}, u32[]{:S(2)}, u32[]{:S(2)}) collective-permute-start(bf16[16,64,128]{2,1,0:T(8,128)(2,1)S(1)} %collective-permute-done.2.s10_ref), channel_id=1, source_target_pairs={{0,1},{1,0},{2,3},{3,2},{4,5},{5,4},{6,7},{7,6},{8,9},{9,8},{10,11... | collective-permute-start | bytes 786440 | tf_op jit(solution)/shard_map/ppermute | solution.py:283
  64.6 0.0 copy-start
  64.6 0.0 copy-start.1
  64.6 0.0 copy-start.2
  64.6 4.7 %collective-permute-start = (bf16[512,1024]{1,0:T(8,128)(2,1)}, bf16[512,1024]{1,0:T(8,128)(2,1)S(1)}, u32[]{:S(2)}, u32[]{:S(2)}) collective-permute-start(bf16[512,1024]{1,0:T(8,128)(2,1)} %get-tuple-element.14), channel_id=1, source_target_pairs={{0,16},{16,32},{32,48},{48,64},{64,80},{80,96},{96,112},{112,128},... | collective-permute-start | bytes 3145736 | tf_op jit(solution)/shard_map/ppermute | solution.py:287
  69.3 0.0 collective-permute-done.1.s01_ref
  69.3 0.0 collective-permute-done.3.s11_ref
  69.3 17.0 %far.1 = bf16[16,72,256]{2,1,0:T(8,128)(2,1)} custom-call(s32[2]{0:T(128)S(1)} %pad_add_fusion.where_ref, bf16[16,72,256]{2,1,0:T(8,128)(2,1)S(1)} %all-to-all-done.got_ref.q_ref, bf16[16,64,128]{2,1,0:T(8,128)(2,1)S(1)} %all_to_all.15.s00_ref, bf16[16,64,128]{2,1,0:T(8,128)(2,1)S(1)} %collective-permute-done.1.s01_ref, ...), custom_call_target="tpu_custom_call" | custom-call | flops 5368709120 | bytes 3145728 | tf_op jit(solution)/shard_map/far/pallas_call | solution.py:289
  86.4 5.0 %all-to-all-start.2 = ((bf16[16,72,256]{2,1,0:T(8,128)(2,1)}), bf16[16,72,256]{2,1,0:T(8,128)(2,1)S(1)}, u32[]{:S(2)}, u32[]{:S(2)}) async-start(bf16[16,72,256]{2,1,0:T(8,128)(2,1)} %far.1), calls=%async_computation.2 | async-start | bytes 1179648 | tf_op jit(solution)/shard_map/all_to_all | solution.py:305
  91.3 0.0 copy-done
  91.3 0.0 copy-done.1
  91.3 0.0 copy-done.2
  91.3 3.1 %near_own.1 = (f32[8,80,512]{2,1,0:T(8,128)S(1)}, f32[8,8,512]{2,1,0:T(8,128)S(1)}) custom-call(s32[1]{0:T(128)} %bitcast.has_ref, bf16[16,72,256]{2,1,0:T(8,128)(2,1)S(1)} %copy-done, bf16[512,512]{1,0:T(8,128)(2,1)S(1)} %bitcast.9, bf16[512,512]{1,0:T(8,128)(2,1)S(1)} %bitcast.11), custom_call_target="tpu_custom_call" | custom-call | flops 1073741824 | bytes 4194304 | tf_op jit(solution)/shard_map/near_own/pallas_call | solution.py:233
  94.5 4.9 %collective-permute-done.rest_0_ = bf16[512,1024]{1,0:T(8,128)(2,1)S(1)} collective-permute-done((bf16[512,1024]{1,0:T(8,128)(2,1)}, bf16[512,1024]{1,0:T(8,128)(2,1)S(1)}, u32[]{:S(2)}, u32[]{:S(2)}) %collective-permute-start) | collective-permute-done | bytes 1048608 | tf_op jit(solution)/shard_map/ppermute | solution.py:287
  99.4 0.0 copy-start.3
  99.4 1.0 copy-done.3
  100.4 0.0 copy-start.4
  100.4 1.2 %copy-done.4 = bf16[512,1024]{1,0:T(8,128)(2,1)S(1)} copy-done((bf16[512,1024]{1,0:T(8,128)(2,1)S(1)}, bf16[512,1024]{1,0:T(8,128)(2,1)}, u32[]{:S(2)}) %copy-start.4) | copy-done | bytes 1048600
  101.6 5.2 %near_prev.1 = (f32[8,80,512]{2,1,0:T(8,128)S(1)}, f32[8,8,512]{2,1,0:T(8,128)S(1)}) custom-call(s32[1]{0:T(128)} %bitcast.has_ref, bf16[16,72,256]{2,1,0:T(8,128)(2,1)S(1)} %copy-done, bf16[512,1024]{1,0:T(8,128)(2,1)S(1)} %copy-done.4, f32[8,80,512]{2,1,0:T(8,128)S(1)} %get-tuple-element.15.rest_1_, f32[8,8,512]{2,1,0:T(8,128)S(1)} %get-tuple-element.16.rest_2_), custom_call_target="tpu_custom_call" | custom-call | flops 1073741824 | bytes 4194304 | tf_op jit(solution)/shard_map/near_prev/pallas_call | solution.py:233
  106.8 0.0 all-to-all-done.2.far_ref
  106.9 1.1 %merge.1 = bf16[512,512]{1,0:T(8,128)(2,1)} custom-call(f32[8,80,512]{2,1,0:T(8,128)S(1)} %get-tuple-element.17.acc_ref, f32[8,8,512]{2,1,0:T(8,128)S(1)} %get-tuple-element.18.peak_ref, bf16[16,72,256]{2,1,0:T(8,128)(2,1)S(1)} %all-to-all-done.2.far_ref), custom_call_target="tpu_custom_call" | custom-call | flops 2097152 | bytes 3145728 | tf_op jit(solution)/shard_map/merge/pallas_call | solution.py:308
Async XLA Ops:
  2.9 15.7 %all-to-all-start = ((bf16[16,72,256]{2,1,0:T(8,128)(2,1)}), bf16[16,72,256]{2,1,0:T(8,128)(2,1)S(1)}, u32[]{:S(2)}, u32[]{:S(2)}) async-start(bf16[16,72,256]{2,1,0:T(8,128)(2,1)} %get-tuple-element.12.qt_ref), calls=%async_computation | async-start | bytes 1179648 | tf_op jit(solution)/shard_map/all_to_all | solution.py:270
  52.3 10.3 %collective-permute-start.2 = (bf16[16,64,128]{2,1,0:T(8,128)(2,1)S(1)}, bf16[16,64,128]{2,1,0:T(8,128)(2,1)S(1)}, u32[]{:S(2)}, u32[]{:S(2)}) collective-permute-start(bf16[16,64,128]{2,1,0:T(8,128)(2,1)S(1)} %all_to_all.15.s00_ref), channel_id=1, source_target_pairs={{0,256},{16,272},{32,288},{48,304},{64,320},{80,336},{96,352},{112... | collective-permute-start | bytes 786440 | tf_op jit(solution)/shard_map/ppermute | solution.py:281
  55.6 13.8 %collective-permute-start.1 = (bf16[16,64,128]{2,1,0:T(8,128)(2,1)S(1)}, bf16[16,64,128]{2,1,0:T(8,128)(2,1)S(1)}, u32[]{:S(2)}, u32[]{:S(2)}) collective-permute-start(bf16[16,64,128]{2,1,0:T(8,128)(2,1)S(1)} %all_to_all.15.s00_ref), channel_id=1, source_target_pairs={{0,1},{1,0},{2,3},{3,2},{4,5},{5,4},{6,7},{7,6},{8,9},{9,8},{10,11... | collective-permute-start | bytes 786440 | tf_op jit(solution)/shard_map/ppermute | solution.py:282
  62.7 6.7 %collective-permute-start.3 = (bf16[16,64,128]{2,1,0:T(8,128)(2,1)S(1)}, bf16[16,64,128]{2,1,0:T(8,128)(2,1)S(1)}, u32[]{:S(2)}, u32[]{:S(2)}) collective-permute-start(bf16[16,64,128]{2,1,0:T(8,128)(2,1)S(1)} %collective-permute-done.2.s10_ref), channel_id=1, source_target_pairs={{0,1},{1,0},{2,3},{3,2},{4,5},{5,4},{6,7},{7,6},{8,9},{9,8},{10,11... | collective-permute-start | bytes 786440 | tf_op jit(solution)/shard_map/ppermute | solution.py:283
  64.6 26.7 %copy-start = (bf16[16,72,256]{2,1,0:T(8,128)(2,1)S(1)}, bf16[16,72,256]{2,1,0:T(8,128)(2,1)}, u32[]{:S(2)}) copy-start(bf16[16,72,256]{2,1,0:T(8,128)(2,1)} %get-tuple-element.12.qt_ref) | copy-start | bytes 1769476
  64.6 26.7 %copy-start.1 = (bf16[1,512,512]{2,1,0:T(8,128)(2,1)S(1)}, bf16[1,512,512]{2,1,0:T(8,128)(2,1)}, u32[]{:S(2)}) copy-start(bf16[1,512,512]{2,1,0:T(8,128)(2,1)} %param.5) | copy-start | bytes 1572868
  64.6 26.7 %copy-start.2 = (bf16[1,512,512]{2,1,0:T(8,128)(2,1)S(1)}, bf16[1,512,512]{2,1,0:T(8,128)(2,1)}, u32[]{:S(2)}) copy-start(bf16[1,512,512]{2,1,0:T(8,128)(2,1)} %param.6) | copy-start | bytes 1572868
  64.6 34.8 %collective-permute-start = (bf16[512,1024]{1,0:T(8,128)(2,1)}, bf16[512,1024]{1,0:T(8,128)(2,1)S(1)}, u32[]{:S(2)}, u32[]{:S(2)}) collective-permute-start(bf16[512,1024]{1,0:T(8,128)(2,1)} %get-tuple-element.14), channel_id=1, source_target_pairs={{0,16},{16,32},{32,48},{48,64},{64,80},{80,96},{96,112},{112,128},... | collective-permute-start | bytes 3145736 | tf_op jit(solution)/shard_map/ppermute | solution.py:287
  86.4 20.5 %all-to-all-start.2 = ((bf16[16,72,256]{2,1,0:T(8,128)(2,1)}), bf16[16,72,256]{2,1,0:T(8,128)(2,1)S(1)}, u32[]{:S(2)}, u32[]{:S(2)}) async-start(bf16[16,72,256]{2,1,0:T(8,128)(2,1)} %far.1), calls=%async_computation.2 | async-start | bytes 1179648 | tf_op jit(solution)/shard_map/all_to_all | solution.py:305
  99.4 1.0 copy-start.3
  100.4 1.2 %copy-start.4 = (bf16[512,1024]{1,0:T(8,128)(2,1)S(1)}, bf16[512,1024]{1,0:T(8,128)(2,1)}, u32[]{:S(2)}) copy-start(bf16[512,1024]{1,0:T(8,128)(2,1)} %copy-done.3) | copy-start | bytes 3145732

commit v2 on v1

--- a/solution.py
+++ b/solution.py
@@ -7,6 +7,7 @@
 from jax.experimental import pallas as pl
 from jax.experimental.pallas import tpu as pltpu
 from jax.sharding import PartitionSpec as P
+
 
 H = 8
 HD = 64
@@ -36,9 +37,14 @@
     return top, acc
 
 
-def prep_kernel(pos_ref, q_ref, k_ref, v_ref, send_ref, kv_ref):
-    kv_ref[:, : H * HD] = k_ref[...]
-    kv_ref[:, H * HD :] = v_ref[...]
+def thirds(value):
+    high = value.astype(bf16)
+    rest = value - high.astype(f32)
+    mid = rest.astype(bf16)
+    return high, mid, (rest - mid.astype(f32)).astype(bf16)
+
+
+def prep_kernel(pos_ref, q_ref, k_ref, v_ref, send_ref):
     slot = lax.broadcasted_iota(jnp.int32, (16, BLK), 0)
     token = lax.broadcasted_iota(jnp.int32, (16, BLK), 1)
     wanted = jnp.full((16, BLK), -1, jnp.int32)
@@ -57,7 +63,7 @@
             send_ref[2 * h + half, HD:] = rows
 
 
-def spread_kernel(where_ref, got_ref, out_ref):
+def pick_kernel(where_ref, got_ref, out_ref):
     odd = where_ref[1] > 0
     pieces = [jnp.where(odd, got_ref[2 * i + 1], got_ref[2 * i]) for i in range(8)]
     rows = jnp.concatenate(pieces, axis=0)
@@ -67,7 +73,9 @@
 
 def near_kernel(own, has_ref, qt_ref, *rest):
     if own:
-        k_ref, v_ref, acc_ref, peak_ref, vt_ref = rest
+        k_ref, v_ref, acc_ref, peak_ref, kv_ref, vt_ref = rest
+        kv_ref[:, : H * HD] = k_ref[...]
+        kv_ref[:, H * HD :] = v_ref[...]
         v_t = v_ref[...].T
     else:
         k_ref, acc_in, peak_in, acc_ref, peak_ref, vt_ref = rest
@@ -110,41 +118,48 @@
     half = where_ref[1]
     y = c // 16
     sets = (s00_ref, s01_ref, s10_ref, s11_ref)
-    part = 256
+    part = 128
     tile = 4 * part
     wide = 2 * HALF
     lane = lax.broadcasted_iota(jnp.int32, (part, 128), 1)
-    row = lax.broadcasted_iota(jnp.int32, (part, 128), 0)
-    age = 64 * ((row % 16) // SUMM) + row // 16 - 32 * lane
-    age = jnp.where(lane < 16, age, -(1 << 20))
-    key_lane = lane >= HD
-    for p in range(4):
+    layer = lax.broadcasted_iota(jnp.int32, (part, 128), 0) // SUMM
+    low = lane < HD
+    shift = jnp.where(lane < 16, 32 * lane, 1 << 20)
+    ages = []
+    for hh in range(2):
+        turned = jnp.where((half ^ hh) > 0, layer ^ 8, layer)
+        ages.append(turned - shift)
+    for gg in range(8):
         for i, ref in enumerate(sets):
-            rows = ref[:, p * 16 : p * 16 + 16].reshape(part, 128)
-            start = 128 * p + 32 * (half ^ (i % 2)) + 16 * (y ^ (i // 2))
-            bias = jnp.where(age <= c - 2 - start, 0.0, NONE).astype(bf16)
-            k_ref[p, i * part : (i + 1) * part] = jnp.where(key_lane, rows, bias)
-            vt_ref[p, :, i * part : (i + 1) * part] = rows.T[:ACC]
-        vt_ref[p, HD:] = jnp.ones((ACC - HD, tile), bf16)
+            at = slice(i * part, (i + 1) * part)
+            rows = ref[:, gg * SUMM : (gg + 1) * SUMM].reshape(part, 128)
+            start = 64 * gg + 32 * (half ^ (i % 2)) + 16 * (y ^ (i // 2))
+            bias = jnp.where(ages[i % 2] <= c - 2 - start, 0.0, NONE).astype(bf16)
+            k_ref[gg, at] = jnp.where(low, bias, rows)
+            vt_ref[gg, :, at] = rows.T[:ACC]
+        vt_ref[gg, HD:] = jnp.ones((ACC - HD, tile), bf16)
     at = lax.broadcasted_iota(jnp.int32, (HD, HALF), 0)
     for g in range(16):
         one_hot = jnp.where(at == g, 1.0, 0.0).astype(bf16)
         cols = slice((g % 2) * HALF, (g % 2 + 1) * HALF)
         qt_ref[g // 2, :, cols] = jnp.concatenate([one_hot, q_ref[g, :HD]], axis=0)
 
-    def scores(pair, p, buf, peak):
-        for i in range(4):
-            piece = dot(k_ref[p, i * part : (i + 1) * part], qt_ref[pair])
-            buf[p, i * part : (i + 1) * part] = piece
-            peak = jnp.maximum(peak, piece.reshape(part // 8, 8, wide).max(0))
+    def scores(pair, first, count, buf, peak):
+        for j in range(count):
+            for i in range(0, tile, 256):
+                piece = dot(k_ref[first + j, i : i + 256], qt_ref[pair])
+                buf[first + j, i : i + 256] = piece
+                peak = jnp.maximum(peak, piece.reshape(32, 8, wide).max(0))
         return peak
 
-    def values(p, buf, top, acc):
+    def values(first, count, buf, top, acc):
         weights = [
-            jnp.exp2((buf[p, i * part : (i + 1) * part] - top) * RATE).astype(bf16)
-            for i in range(4)
+            jnp.exp2((buf[first + j, i : i + 256] - top) * RATE).astype(bf16)
+            for j in range(count)
+            for i in range(0, tile, 256)
         ]
-        return acc + dot(vt_ref[p], jnp.concatenate(weights, axis=0))
+        rows = [vt_ref[first + j] for j in range(count)]
+        return acc + dot(jnp.concatenate(rows, axis=1), jnp.concatenate(weights, axis=0))
 
     def finish(pair, top, acc):
         total = acc[HD : HD + 1]
@@ -152,11 +167,7 @@
         safe = jnp.where(some, total, 1.0)
         result = (acc[:HD] * (1.0 / safe)).astype(bf16)
         level = jnp.where(some, top * RATE + jnp.log2(safe), NONE)
-        high = level.astype(bf16)
-        rest = level - high.astype(f32)
-        mid = rest.astype(bf16)
-        low = (rest - mid.astype(f32)).astype(bf16)
-        stats = jnp.concatenate([high, mid, low, jnp.zeros((SEND - HD - 3, wide), bf16)], axis=0)
+        stats = jnp.concatenate([*thirds(level), jnp.zeros((SEND - HD - 3, wide), bf16)], axis=0)
         for j in range(2):
             cols = slice(j * HALF, (j + 1) * HALF)
             out_ref[2 * pair + j, :HD] = result[:, cols]
@@ -165,27 +176,29 @@
     floor = jnp.full((8, wide), FLOOR, f32)
     empty = jnp.zeros((ACC, wide), f32)
 
-    def turn(pair, count, more, this, other, peak):
+    def turn(pair, tiles, this, other, peak):
         top = peak.max(0, keepdims=True)
         later = jnp.minimum(pair + 1, 7)
 
         def both(p, carry):
             acc, ahead = carry
-            ahead = scores(later, p, other, ahead)
-            acc = values(p, this, top, acc)
+            ahead = scores(later, 2 * p, 2, other, ahead)
+            acc = values(2 * p, 2, this, top, acc)
             return acc, ahead
 
-        acc, ahead = lax.fori_loop(0, count, both, (empty, floor))
-        if more:
-            ahead = scores(later, jnp.minimum(count, 3), other, ahead)
-        finish(pair, top, acc)
+        return later, top, *lax.fori_loop(0, tiles, both, (empty, floor))
+
+    def quad(i, peak):
+        later, top, acc, ahead = turn(2 * i, i, even_ref, odd_ref, peak)
+        ahead = scores(later, 2 * i, 2, odd_ref, ahead)
+        acc = values(2 * i, 1, even_ref, top, acc)
+        finish(2 * i, top, acc)
+        later, top, acc, ahead = turn(2 * i + 1, i + 1, odd_ref, even_ref, ahead)
+        ahead = scores(later, jnp.minimum(2 * i + 2, 7), 1, even_ref, ahead)
+        finish(2 * i + 1, top, acc)
         return ahead
 
-    def quad(i, peak):
-        peak = turn(2 * i, i + 1, False, even_ref, odd_ref, peak)
-        return turn(2 * i + 1, i + 1, True, odd_ref, even_ref, peak)
-
-    lax.fori_loop(0, 4, quad, scores(0, 0, even_ref, floor))
+    lax.fori_loop(0, 4, quad, scores(0, 0, 1, even_ref, floor))
 
 
 def merge_kernel(acc_ref, peak_ref, far_ref, out_ref):
@@ -230,11 +243,13 @@
         jax.ShapeDtypeStruct((H, ACC, BLK), f32),
         jax.ShapeDtypeStruct((H, 8, BLK), f32),
     )
+    if own:
+        shapes += (jax.ShapeDtypeStruct((BLK, 2 * H * HD), bf16),)
     return pl.pallas_call(
         functools.partial(near_kernel, own),
         out_shape=shapes,
         in_specs=[SMEM] + vmem(len(args)),
-        out_specs=tuple(vmem(2)),
+        out_specs=tuple(vmem(len(shapes))),
         scratch_shapes=[pltpu.VMEM((H, ACC, BLK), bf16)],
         compiler_params=LIMIT,
         cost_estimate=cost(2 * H * BLK * BLK * 256, 4 << 20, H * BLK * BLK),
@@ -247,42 +262,44 @@
     g = lax.axis_index("grp")
     groups, per_group = lax.axis_size("grp"), lax.axis_size("ctx")
     layers = per_group // 2
-    same_y = [[y * layers + z for z in range(layers)] for y in range(2)]
+    rings = [
+        [(y * layers + (z + layers // 2 * (i % 2)) % layers) * groups + i for z in range(layers)]
+        for y in range(2)
+        for i in range(groups)
+    ]
     other_y = [(i, (i + layers) % per_group) for i in range(per_group)]
     other_core = [(i, i ^ 1) for i in range(groups)]
     q, k, v = queries[0], keys[0], values[0]
 
     where = jnp.stack([c, g % 2]).astype(jnp.int32)
     has = jnp.where(c + g > 0, 1, 0).astype(jnp.int32)[None]
-    send, kv = pl.pallas_call(
+    send = pl.pallas_call(
         prep_kernel,
-        out_shape=(
-            jax.ShapeDtypeStruct((groups, SEND, HALF), bf16),
-            jax.ShapeDtypeStruct((BLK, 2 * H * HD), bf16),
-        ),
+        out_shape=jax.ShapeDtypeStruct((groups, SEND, HALF), bf16),
         in_specs=[SMEM] + vmem(3),
-        out_specs=tuple(vmem(2)),
+        out_specs=vmem(1)[0],
         cost_estimate=cost(4 * 16 * BLK * BLK, 3 << 20),
         name="prep",
     )(summary_pos[0, 0], q, k, v)
-    carried = near(True, has, send, k, v)
+    *carried, kv = near(True, has, send, k, v)
 
     got = lax.all_to_all(send, "grp", 0, 0, tiled=True)
     mine = pl.pallas_call(
-        spread_kernel,
+        pick_kernel,
         out_shape=jax.ShapeDtypeStruct((layers, 64, 128), bf16),
         grid=(1,),
         in_specs=[SMEM, pl.BlockSpec((groups, SUMM, 128), lambda i: (0, HD // SUMM, 0))],
         out_specs=pl.BlockSpec((layers, 64, 128), lambda i: (0, 0, 0)),
         compiler_params=LIMIT,
-        name="spread",
+        name="pick",
     )(where, got)
-    s00 = lax.all_to_all(mine, "ctx", 0, 0, tiled=True, axis_index_groups=same_y)
+    both_axes = ("ctx", "grp")
+    s00 = lax.all_to_all(mine, both_axes, 0, 0, tiled=True, axis_index_groups=rings)
     s10 = lax.ppermute(s00, "ctx", other_y)
     s01 = lax.ppermute(s00, "grp", other_core)
     s11 = lax.ppermute(s10, "grp", other_core)
 
-    kv, unused = lax.optimization_barrier((kv, s00))
+    kv, _ = lax.optimization_barrier((kv, s00))
     flat = [t * groups + s for s in range(groups) for t in range(per_group)]
     kv_prev = lax.ppermute(kv, ("ctx", "grp"), list(zip(flat[:-1], flat[1:])))
 
@@ -292,11 +309,11 @@
         in_specs=[SMEM] + vmem(5),
         out_specs=vmem(1)[0],
         scratch_shapes=[
-            pltpu.VMEM((4, ACC, 1024), bf16),
-            pltpu.VMEM((4, 1024, 128), bf16),
+            pltpu.VMEM((8, ACC, 512), bf16),
+            pltpu.VMEM((8, 512, 128), bf16),
             pltpu.VMEM((groups // 2, 128, 2 * HALF), bf16),
-            pltpu.VMEM((4, 1024, 2 * HALF), f32),
-            pltpu.VMEM((4, 1024, 2 * HALF), f32),
+            pltpu.VMEM((8, 512, 2 * HALF), f32),
+            pltpu.VMEM((8, 512, 2 * HALF), f32),
         ],
         compiler_params=pltpu.CompilerParams(vmem_limit_bytes=32 << 20),
         cost_estimate=cost(2 * 40 * 1024 * HALF * 256, 3 << 20, 40 * 1024 * HALF),

time: 108 us -> 113 us (1.046)
  the two profiles are of different devices: /device:TPU:10 before, /device:TPU:1 now
where the time goes in v2:
time: 113 us; the launch traced here: 112 us
  Pallas kernels  29 us (26%)
  blocking collectives  28.7 us (25%)
  starting transfers between devices  25 us (22%)
  waiting for transfers between devices  22.5 us (20%)
  local copies, waits for them, and re-layouts  6.16 us (5%)
    all_to_all x1, blocking collectives, shards(): lax.all_to_all(mine, both_axes, 0, 0, tiled=True, axis_index_groups=rings)  28.7 us
    pallas_call x1, Pallas kernels, shards(): pl.pallas_call(far_kernel, out_shape=jax.ShapeDtypeStruct((groups, SEND,...  16.3 us
    all_to_all x1, waiting for transfers between devices, shards(): got = lax.all_to_all(send, 'grp', 0, 0, tiled=True)  12 us
    all_to_all x1, starting transfers between devices, shards(): got = lax.all_to_all(send, 'grp', 0, 0, tiled=True)  10.3 us
    pallas_call x2, Pallas kernels, near(): pl.pallas_call(functools.partial(near_kernel, own), out_shape=shapes, in_...  8.4 us
    unnamed x18, local copies, waits for them, and re-layouts  6.16 us
    ppermute x1, waiting for transfers between devices, shards(): kv_prev = lax.ppermute(kv, ('ctx', 'grp'), list(zip(flat[:-1], flat[1:])))  5.98 us
    all_to_all x1, starting transfers between devices, shards(): far = lax.all_to_all(partial, 'grp', 0, 0, tiled=True)  4.57 us
  transfers between devices with their start and end apart: 6, of which 3 were waited for; matrix products, arithmetic and copies ran while one was open for 0% of the time, Pallas kernels for 22%

profile of v2, /device:TPU:1, one launch (start us, length us, event | category | flops | bytes accessed | tf_op | source)
XLA Modules:
  0.0 111.6 jit_solution(16619400479145277509)
XLA Ops:
  0.0 2.5 %prep.1.qt_ref = bf16[16,72,256]{2,1,0:T(8,128)(2,1)} custom-call(s32[8]{0:T(128)} %bitcast.13, bf16[512,512]{1,0:T(8,128)(2,1)} %bitcast.12, bf16[512,512]{1,0:T(8,128)(2,1)} %bitcast.8, bf16[512,512]{1,0:T(8,128)(2,1)} %bitcast.10), custom_call_target="tpu_custom_call" | custom-call | flops 16777216 | bytes 3145728 | tf_op jit(solution)/shard_map/prep/pallas_call | solution.py:276
  2.5 0.0 copy-start
  2.5 0.0 copy-start.1
  2.5 0.0 copy-start.2
  2.5 10.3 %all-to-all-start = ((bf16[16,72,256]{2,1,0:T(8,128)(2,1)}), bf16[16,72,256]{2,1,0:T(8,128)(2,1)S(1)}, u32[]{:S(2)}, u32[]{:S(2)}) async-start(bf16[16,72,256]{2,1,0:T(8,128)(2,1)} %prep.1.qt_ref), calls=%async_computation | async-start | bytes 1179648 | tf_op jit(solution)/shard_map/all_to_all | solution.py:286
  12.9 0.1 pad_add_fusion.where_ref
  13.0 12.0 %all-to-all-done.got_ref.q_ref = bf16[16,72,256]{2,1,0:T(8,128)(2,1)S(1)} async-done(((bf16[16,72,256]{2,1,0:T(8,128)(2,1)}), bf16[16,72,256]{2,1,0:T(8,128)(2,1)S(1)}, u32[]{:S(2)}, u32[]{:S(2)}) %all-to-all-start) | async-done | bytes 589856 | tf_op jit(solution)/shard_map/all_to_all | solution.py:286
  24.9 0.6 pick.1
  25.5 28.7 %all_to_all.15.s00_ref = bf16[16,64,128]{2,1,0:T(8,128)(2,1)S(1)} all-to-all(bf16[16,64,128]{2,1,0:T(8,128)(2,1)S(1)} %pick.1), channel_id=1, replica_groups={{0,16,32,48,64,80,96,112,128,144,160,176,192,208,224,240},{129,145,161,..., dimensions={0} | all-to-all | bytes 524288 | tf_op jit(solution)/shard_map/all_to_all | solution.py:297
  54.3 2.3 %collective-permute-start.2 = (bf16[16,64,128]{2,1,0:T(8,128)(2,1)S(1)}, bf16[16,64,128]{2,1,0:T(8,128)(2,1)}, u32[]{:S(2)}, u32[]{:S(2)}) collective-permute-start(bf16[16,64,128]{2,1,0:T(8,128)(2,1)S(1)} %all_to_all.15.s00_ref), channel_id=1, source_target_pairs={{0,256},{16,272},{32,288},{48,304},{64,320},{80,336},{96,352},{112... | collective-permute-start | bytes 786440 | tf_op jit(solution)/shard_map/ppermute | solution.py:298
  56.6 2.6 %collective-permute-start.1 = (bf16[16,64,128]{2,1,0:T(8,128)(2,1)S(1)}, bf16[16,64,128]{2,1,0:T(8,128)(2,1)}, u32[]{:S(2)}, u32[]{:S(2)}) collective-permute-start(bf16[16,64,128]{2,1,0:T(8,128)(2,1)S(1)} %all_to_all.15.s00_ref), channel_id=1, source_target_pairs={{0,1},{1,0},{2,3},{3,2},{4,5},{5,4},{6,7},{7,6},{8,9},{9,8},{10,11... | collective-permute-start | bytes 786440 | tf_op jit(solution)/shard_map/ppermute | solution.py:299
  59.2 4.6 %collective-permute-done.2.s10_ref = bf16[16,64,128]{2,1,0:T(8,128)(2,1)} collective-permute-done((bf16[16,64,128]{2,1,0:T(8,128)(2,1)S(1)}, bf16[16,64,128]{2,1,0:T(8,128)(2,1)}, u32[]{:S(2)}, u32[]{:S(2)}) %collective-permute-start.2) | collective-permute-done | bytes 262176 | tf_op jit(solution)/shard_map/ppermute | solution.py:298
  63.7 3.1 %collective-permute-start.3 = (bf16[16,64,128]{2,1,0:T(8,128)(2,1)}, bf16[16,64,128]{2,1,0:T(8,128)(2,1)}, u32[]{:S(2)}, u32[]{:S(2)}) collective-permute-start(bf16[16,64,128]{2,1,0:T(8,128)(2,1)} %collective-permute-done.2.s10_ref), channel_id=1, source_target_pairs={{0,1},{1,0},{2,3},{3,2},{4,5},{5,4},{6,7},{7,6},{8,9},{9,8},{10,11... | collective-permute-start | bytes 786440 | tf_op jit(solution)/shard_map/ppermute | solution.py:300
  66.9 0.0 copy-done
  66.9 0.0 copy-done.1
  66.9 0.0 copy-done.2
  66.9 3.2 %near_own.1 = (f32[8,80,512]{2,1,0:T(8,128)S(1)}, f32[8,8,512]{2,1,0:T(8,128)S(1)}, bf16[512,1024]{1,0:T(8,128)(2,1)S(1)}) custom-call(s32[1]{0:T(128)} %bitcast.has_ref, bf16[16,72,256]{2,1,0:T(8,128)(2,1)S(1)} %copy-done, bf16[512,512]{1,0:T(8,128)(2,1)S(1)} %bitcast.9, bf16[512,512]{1,0:T(8,128)(2,1)S(1)} %bitcast.11), custom_call_target="tpu_custom_call" | custom-call | flops 1073741824 | bytes 4194304 | tf_op jit(solution)/shard_map/near_own/pallas_call | solution.py:248
  70.1 0.0 copy-start.5
  70.1 1.1 copy-done.5
  71.2 0.0 copy-start.7
  71.2 0.7 copy-done.7
  71.9 2.1 %collective-permute-start = (bf16[512,1024]{1,0:T(8,128)(2,1)S(1)}, bf16[512,1024]{1,0:T(8,128)(2,1)S(1)}, u32[]{:S(2)}, u32[]{:S(2)}) collective-permute-start(bf16[512,1024]{1,0:T(8,128)(2,1)S(1)} %get-tuple-element.12), channel_id=1, source_target_pairs={{0,16},{16,32},{32,48},{48,64},{64,80},{80,96},{96,112},{112,128},... | collective-permute-start | bytes 3145736 | tf_op jit(solution)/shard_map/ppermute | solution.py:304
  73.9 0.0 collective-permute-done.1.s01_ref
  73.9 0.0 collective-permute-done.3.s11_ref
  73.9 16.3 %far.1 = bf16[16,72,256]{2,1,0:T(8,128)(2,1)} custom-call(s32[2]{0:T(128)S(1)} %pad_add_fusion.where_ref, bf16[16,72,256]{2,1,0:T(8,128)(2,1)S(1)} %all-to-all-done.got_ref.q_ref, bf16[16,64,128]{2,1,0:T(8,128)(2,1)S(1)} %all_to_all.15.s00_ref, bf16[16,64,128]{2,1,0:T(8,128)(2,1)} %collective-permute-done.1.s01_ref, ...), custom_call_target="tpu_custom_call" | custom-call | flops 5368709120 | bytes 3145728 | tf_op jit(solution)/shard_map/far/pallas_call | solution.py:306
  90.3 4.6 %all-to-all-start.2 = ((bf16[16,72,256]{2,1,0:T(8,128)(2,1)}), bf16[16,72,256]{2,1,0:T(8,128)(2,1)S(1)}, u32[]{:S(2)}, u32[]{:S(2)}) async-start(bf16[16,72,256]{2,1,0:T(8,128)(2,1)} %far.1), calls=%async_computation.2 | async-start | bytes 1179648 | tf_op jit(solution)/shard_map/all_to_all | solution.py:322
  94.8 6.0 %collective-permute-done.rest_0_ = bf16[512,1024]{1,0:T(8,128)(2,1)S(1)} collective-permute-done((bf16[512,1024]{1,0:T(8,128)(2,1)S(1)}, bf16[512,1024]{1,0:T(8,128)(2,1)S(1)}, u32[]{:S(2)}, u32[]{:S(2)}) %collective-permute-start) | collective-permute-done | bytes 1048608 | tf_op jit(solution)/shard_map/ppermute | solution.py:304
  100.8 0.0 copy-start.3
  100.8 1.0 copy-done.3
  101.8 0.0 copy-start.4
  101.8 1.2 %copy-done.4 = bf16[512,1024]{1,0:T(8,128)(2,1)S(1)} copy-done((bf16[512,1024]{1,0:T(8,128)(2,1)S(1)}, bf16[512,1024]{1,0:T(8,128)(2,1)}, u32[]{:S(2)}) %copy-start.4) | copy-done | bytes 1048600
  103.0 0.0 copy-start.6
  103.0 1.3 %copy-done.6 = f32[8,80,512]{2,1,0:T(8,128)S(1)} copy-done((f32[8,80,512]{2,1,0:T(8,128)S(1)}, f32[8,80,512]{2,1,0:T(8,128)}, u32[]{:S(2)}) %copy-start.6) | copy-done | bytes 1310744
  104.3 0.0 copy-start.8
  104.3 0.9 copy-done.8
  105.2 5.2 %near_prev.1 = (f32[8,80,512]{2,1,0:T(8,128)S(1)}, f32[8,8,512]{2,1,0:T(8,128)S(1)}) custom-call(s32[1]{0:T(128)} %bitcast.has_ref, bf16[16,72,256]{2,1,0:T(8,128)(2,1)S(1)} %copy-done, bf16[512,1024]{1,0:T(8,128)(2,1)S(1)} %copy-done.4, f32[8,80,512]{2,1,0:T(8,128)S(1)} %copy-done.6, f32[8,8,512]{2,1,0:T(8,128)S(1)} %copy-done.8), custom_call_target="tpu_custom_call" | custom-call | flops 1073741824 | bytes 4194304 | tf_op jit(solution)/shard_map/near_prev/pallas_call | solution.py:248
  110.5 0.0 all-to-all-done.2.far_ref
  110.5 1.1 %merge.1 = bf16[512,512]{1,0:T(8,128)(2,1)} custom-call(f32[8,80,512]{2,1,0:T(8,128)S(1)} %get-tuple-element.15.acc_ref, f32[8,8,512]{2,1,0:T(8,128)S(1)} %get-tuple-element.16.peak_ref, bf16[16,72,256]{2,1,0:T(8,128)(2,1)S(1)} %all-to-all-done.2.far_ref), custom_call_target="tpu_custom_call" | custom-call | flops 2097152 | bytes 3145728 | tf_op jit(solution)/shard_map/merge/pallas_call | solution.py:325
Async XLA Ops:
  2.5 64.4 %copy-start = (bf16[16,72,256]{2,1,0:T(8,128)(2,1)S(1)}, bf16[16,72,256]{2,1,0:T(8,128)(2,1)}, u32[]{:S(2)}) copy-start(bf16[16,72,256]{2,1,0:T(8,128)(2,1)} %prep.1.qt_ref) | copy-start | bytes 1769476
  2.5 64.4 %copy-start.1 = (bf16[1,512,512]{2,1,0:T(8,128)(2,1)S(1)}, bf16[1,512,512]{2,1,0:T(8,128)(2,1)}, u32[]{:S(2)}) copy-start(bf16[1,512,512]{2,1,0:T(8,128)(2,1)} %param.5) | copy-start | bytes 1572868
  2.5 64.4 %copy-start.2 = (bf16[1,512,512]{2,1,0:T(8,128)(2,1)S(1)}, bf16[1,512,512]{2,1,0:T(8,128)(2,1)}, u32[]{:S(2)}) copy-start(bf16[1,512,512]{2,1,0:T(8,128)(2,1)} %param.6) | copy-start | bytes 1572868
  2.5 22.4 %all-to-all-start = ((bf16[16,72,256]{2,1,0:T(8,128)(2,1)}), bf16[16,72,256]{2,1,0:T(8,128)(2,1)S(1)}, u32[]{:S(2)}, u32[]{:S(2)}) async-start(bf16[16,72,256]{2,1,0:T(8,128)(2,1)} %prep.1.qt_ref), calls=%async_computation | async-start | bytes 1179648 | tf_op jit(solution)/shard_map/all_to_all | solution.py:286
  54.3 9.5 %collective-permute-start.2 = (bf16[16,64,128]{2,1,0:T(8,128)(2,1)S(1)}, bf16[16,64,128]{2,1,0:T(8,128)(2,1)}, u32[]{:S(2)}, u32[]{:S(2)}) collective-permute-start(bf16[16,64,128]{2,1,0:T(8,128)(2,1)S(1)} %all_to_all.15.s00_ref), channel_id=1, source_target_pairs={{0,256},{16,272},{32,288},{48,304},{64,320},{80,336},{96,352},{112... | collective-permute-start | bytes 786440 | tf_op jit(solution)/shard_map/ppermute | solution.py:298
  56.6 17.3 %collective-permute-start.1 = (bf16[16,64,128]{2,1,0:T(8,128)(2,1)S(1)}, bf16[16,64,128]{2,1,0:T(8,128)(2,1)}, u32[]{:S(2)}, u32[]{:S(2)}) collective-permute-start(bf16[16,64,128]{2,1,0:T(8,128)(2,1)S(1)} %all_to_all.15.s00_ref), channel_id=1, source_target_pairs={{0,1},{1,0},{2,3},{3,2},{4,5},{5,4},{6,7},{7,6},{8,9},{9,8},{10,11... | collective-permute-start | bytes 786440 | tf_op jit(solution)/shard_map/ppermute | solution.py:299
  63.7 10.2 %collective-permute-start.3 = (bf16[16,64,128]{2,1,0:T(8,128)(2,1)}, bf16[16,64,128]{2,1,0:T(8,128)(2,1)}, u32[]{:S(2)}, u32[]{:S(2)}) collective-permute-start(bf16[16,64,128]{2,1,0:T(8,128)(2,1)} %collective-permute-done.2.s10_ref), channel_id=1, source_target_pairs={{0,1},{1,0},{2,3},{3,2},{4,5},{5,4},{6,7},{7,6},{8,9},{9,8},{10,11... | collective-permute-start | bytes 786440 | tf_op jit(solution)/shard_map/ppermute | solution.py:300
  70.1 1.1 copy-start.5
  71.2 0.7 copy-start.7
  71.9 29.0 %collective-permute-start = (bf16[512,1024]{1,0:T(8,128)(2,1)S(1)}, bf16[512,1024]{1,0:T(8,128)(2,1)S(1)}, u32[]{:S(2)}, u32[]{:S(2)}) collective-permute-start(bf16[512,1024]{1,0:T(8,128)(2,1)S(1)} %get-tuple-element.12), channel_id=1, source_target_pairs={{0,16},{16,32},{32,48},{48,64},{64,80},{80,96},{96,112},{112,128},... | collective-permute-start | bytes 3145736 | tf_op jit(solution)/shard_map/ppermute | solution.py:304
  90.3 20.2 %all-to-all-start.2 = ((bf16[16,72,256]{2,1,0:T(8,128)(2,1)}), bf16[16,72,256]{2,1,0:T(8,128)(2,1)S(1)}, u32[]{:S(2)}, u32[]{:S(2)}) async-start(bf16[16,72,256]{2,1,0:T(8,128)(2,1)} %far.1), calls=%async_computation.2 | async-start | bytes 1179648 | tf_op jit(solution)/shard_map/all_to_all | solution.py:322
  100.8 1.0 copy-start.3
  101.8 1.2 %copy-start.4 = (bf16[512,1024]{1,0:T(8,128)(2,1)S(1)}, bf16[512,1024]{1,0:T(8,128)(2,1)}, u32[]{:S(2)}) copy-start(bf16[512,1024]{1,0:T(8,128)(2,1)} %copy-done.3) | copy-start | bytes 3145732
  103.0 1.3 %copy-start.6 = (f32[8,80,512]{2,1,0:T(8,128)S(1)}, f32[8,80,512]{2,1,0:T(8,128)}, u32[]{:S(2)}) copy-start(f32[8,80,512]{2,1,0:T(8,128)} %copy-done.5) | copy-start | bytes 3932164
  104.3 0.9 copy-start.8

commit v3 on v2

--- a/solution.py
+++ b/solution.py
@@ -65,7 +65,8 @@
 
 def pick_kernel(where_ref, got_ref, out_ref):
     odd = where_ref[1] > 0
-    pieces = [jnp.where(odd, got_ref[2 * i + 1], got_ref[2 * i]) for i in range(8)]
+    own = [got_ref[i, HD:, :128] for i in range(16)]
+    pieces = [jnp.where(odd, own[2 * i + 1], own[2 * i]) for i in range(8)]
     rows = jnp.concatenate(pieces, axis=0)
     for z in range(out_ref.shape[0]):
         out_ref[z] = rows
@@ -178,7 +179,7 @@
 
     def turn(pair, tiles, this, other, peak):
         top = peak.max(0, keepdims=True)
-        later = jnp.minimum(pair + 1, 7)
+        later = pair + 1
 
         def both(p, carry):
             acc, ahead = carry
@@ -188,17 +189,23 @@
 
         return later, top, *lax.fori_loop(0, tiles, both, (empty, floor))
 
-    def quad(i, peak):
+    def even(i, peak):
         later, top, acc, ahead = turn(2 * i, i, even_ref, odd_ref, peak)
         ahead = scores(later, 2 * i, 2, odd_ref, ahead)
         acc = values(2 * i, 1, even_ref, top, acc)
         finish(2 * i, top, acc)
-        later, top, acc, ahead = turn(2 * i + 1, i + 1, odd_ref, even_ref, ahead)
-        ahead = scores(later, jnp.minimum(2 * i + 2, 7), 1, even_ref, ahead)
+        return ahead
+
+    def odd(i, peak):
+        later, top, acc, ahead = turn(2 * i + 1, i + 1, odd_ref, even_ref, peak)
+        ahead = scores(later, 2 * i + 2, 1, even_ref, ahead)
         finish(2 * i + 1, top, acc)
         return ahead
 
-    lax.fori_loop(0, 4, quad, scores(0, 0, 1, even_ref, floor))
+    peak = scores(0, 0, 1, even_ref, floor)
+    peak = lax.fori_loop(0, 3, lambda i, peak: odd(i, even(i, peak)), peak)
+    top = even(3, peak).max(0, keepdims=True)
+    finish(7, top, lax.fori_loop(0, 2, lambda p, acc: values(4 * p, 4, odd_ref, top, acc), empty))
 
 
 def merge_kernel(acc_ref, peak_ref, far_ref, out_ref):
@@ -287,9 +294,8 @@
     mine = pl.pallas_call(
         pick_kernel,
         out_shape=jax.ShapeDtypeStruct((layers, 64, 128), bf16),
-        grid=(1,),
-        in_specs=[SMEM, pl.BlockSpec((groups, SUMM, 128), lambda i: (0, HD // SUMM, 0))],
-        out_specs=pl.BlockSpec((layers, 64, 128), lambda i: (0, 0, 0)),
+        in_specs=[SMEM] + vmem(1),
+        out_specs=vmem(1)[0],
         compiler_params=LIMIT,
         name="pick",
     )(where, got)

time: 113 us -> 114 us (level); the launches traced: 112 us -> 111 us
  Pallas kernels: 29 us -> 27.7 us
    pallas_call x1, Pallas kernels: 16.3 us -> 15.1 us  [shards(): pl.pallas_call(far_kernel, out_shape=jax.ShapeDtypeStruct((groups, SEND,...]
  transfers between devices with their start and end apart: 6 -> 6, of which waited for: 3 -> 3; matrix products, arithmetic and copies ran while one was open for 0% -> 0% of each run, Pallas kernels for 22% -> 21%
where the time goes in v3:
time: 114 us; the launch traced here: 111 us
  blocking collectives  28.7 us (25%)
  Pallas kernels  27.7 us (24%)
  starting transfers between devices  25 us (22%)
  waiting for transfers between devices  23.6 us (21%)
  local copies, waits for them, and re-layouts  6.16 us (5%)
    all_to_all x1, blocking collectives, shards(): lax.all_to_all(mine, both_axes, 0, 0, tiled=True, axis_index_groups=rings)  28.7 us
    pallas_call x1, Pallas kernels, shards(): pl.pallas_call(far_kernel, out_shape=jax.ShapeDtypeStruct((groups, SEND,...  15.1 us
    all_to_all x1, waiting for transfers between devices, shards(): got = lax.all_to_all(send, 'grp', 0, 0, tiled=True)  12 us
    all_to_all x1, starting transfers between devices, shards(): got = lax.all_to_all(send, 'grp', 0, 0, tiled=True)  10.3 us
    pallas_call x2, Pallas kernels, near(): pl.pallas_call(functools.partial(near_kernel, own), out_shape=shapes, in_...  8.4 us
    ppermute x1, waiting for transfers between devices, shards(): kv_prev = lax.ppermute(kv, ('ctx', 'grp'), list(zip(flat[:-1], flat[1:])))  7.07 us
    unnamed x18, local copies, waits for them, and re-layouts  6.16 us
    all_to_all x1, starting transfers between devices, shards(): far = lax.all_to_all(partial, 'grp', 0, 0, tiled=True)  4.58 us
  transfers between devices with their start and end apart: 6, of which 3 were waited for; matrix products, arithmetic and copies ran while one was open for 0% of the time, Pallas kernels for 21%

profile of v3, /device:TPU:1, one launch (start us, length us, event | category | flops | bytes accessed | tf_op | source)
XLA Modules:
  0.0 111.5 jit_solution(2401666559482566390)
XLA Ops:
  0.0 2.5 %prep.1.qt_ref = bf16[16,72,256]{2,1,0:T(8,128)(2,1)} custom-call(s32[8]{0:T(128)} %bitcast.13, bf16[512,512]{1,0:T(8,128)(2,1)} %bitcast.12, bf16[512,512]{1,0:T(8,128)(2,1)} %bitcast.8, bf16[512,512]{1,0:T(8,128)(2,1)} %bitcast.10), custom_call_target="tpu_custom_call" | custom-call | flops 16777216 | bytes 3145728 | tf_op jit(solution)/shard_map/prep/pallas_call | solution.py:283
  2.5 0.0 copy-start
  2.5 0.0 copy-start.1
  2.5 0.0 copy-start.2
  2.5 10.3 %all-to-all-start = ((bf16[16,72,256]{2,1,0:T(8,128)(2,1)}), bf16[16,72,256]{2,1,0:T(8,128)(2,1)S(1)}, u32[]{:S(2)}, u32[]{:S(2)}) async-start(bf16[16,72,256]{2,1,0:T(8,128)(2,1)} %prep.1.qt_ref), calls=%async_computation | async-start | bytes 1179648 | tf_op jit(solution)/shard_map/all_to_all | solution.py:293
  12.9 0.1 pad_add_fusion.where_ref
  13.0 12.0 %all-to-all-done.got_ref.q_ref = bf16[16,72,256]{2,1,0:T(8,128)(2,1)S(1)} async-done(((bf16[16,72,256]{2,1,0:T(8,128)(2,1)}), bf16[16,72,256]{2,1,0:T(8,128)(2,1)S(1)}, u32[]{:S(2)}, u32[]{:S(2)}) %all-to-all-start) | async-done | bytes 589856 | tf_op jit(solution)/shard_map/all_to_all | solution.py:293
  24.9 0.6 pick.1
  25.5 28.7 %all_to_all.15.s00_ref = bf16[16,64,128]{2,1,0:T(8,128)(2,1)S(1)} all-to-all(bf16[16,64,128]{2,1,0:T(8,128)(2,1)S(1)} %pick.1), channel_id=1, replica_groups={{0,16,32,48,64,80,96,112,128,144,160,176,192,208,224,240},{129,145,161,..., dimensions={0} | all-to-all | bytes 524288 | tf_op jit(solution)/shard_map/all_to_all | solution.py:303
  54.3 2.3 %collective-permute-start.2 = (bf16[16,64,128]{2,1,0:T(8,128)(2,1)S(1)}, bf16[16,64,128]{2,1,0:T(8,128)(2,1)}, u32[]{:S(2)}, u32[]{:S(2)}) collective-permute-start(bf16[16,64,128]{2,1,0:T(8,128)(2,1)S(1)} %all_to_all.15.s00_ref), channel_id=1, source_target_pairs={{0,256},{16,272},{32,288},{48,304},{64,320},{80,336},{96,352},{112... | collective-permute-start | bytes 786440 | tf_op jit(solution)/shard_map/ppermute | solution.py:304
  56.6 2.6 %collective-permute-start.1 = (bf16[16,64,128]{2,1,0:T(8,128)(2,1)S(1)}, bf16[16,64,128]{2,1,0:T(8,128)(2,1)}, u32[]{:S(2)}, u32[]{:S(2)}) collective-permute-start(bf16[16,64,128]{2,1,0:T(8,128)(2,1)S(1)} %all_to_all.15.s00_ref), channel_id=1, source_target_pairs={{0,1},{1,0},{2,3},{3,2},{4,5},{5,4},{6,7},{7,6},{8,9},{9,8},{10,11... | collective-permute-start | bytes 786440 | tf_op jit(solution)/shard_map/ppermute | solution.py:305
  59.2 4.6 %collective-permute-done.2.s10_ref = bf16[16,64,128]{2,1,0:T(8,128)(2,1)} collective-permute-done((bf16[16,64,128]{2,1,0:T(8,128)(2,1)S(1)}, bf16[16,64,128]{2,1,0:T(8,128)(2,1)}, u32[]{:S(2)}, u32[]{:S(2)}) %collective-permute-start.2) | collective-permute-done | bytes 262176 | tf_op jit(solution)/shard_map/ppermute | solution.py:304
  63.7 3.1 %collective-permute-start.3 = (bf16[16,64,128]{2,1,0:T(8,128)(2,1)}, bf16[16,64,128]{2,1,0:T(8,128)(2,1)}, u32[]{:S(2)}, u32[]{:S(2)}) collective-permute-start(bf16[16,64,128]{2,1,0:T(8,128)(2,1)} %collective-permute-done.2.s10_ref), channel_id=1, source_target_pairs={{0,1},{1,0},{2,3},{3,2},{4,5},{5,4},{6,7},{7,6},{8,9},{9,8},{10,11... | collective-permute-start | bytes 786440 | tf_op jit(solution)/shard_map/ppermute | solution.py:306
  66.9 0.0 copy-done
  66.9 0.0 copy-done.1
  66.9 0.0 copy-done.2
  66.9 3.2 %near_own.1 = (f32[8,80,512]{2,1,0:T(8,128)S(1)}, f32[8,8,512]{2,1,0:T(8,128)S(1)}, bf16[512,1024]{1,0:T(8,128)(2,1)S(1)}) custom-call(s32[1]{0:T(128)} %bitcast.has_ref, bf16[16,72,256]{2,1,0:T(8,128)(2,1)S(1)} %copy-done, bf16[512,512]{1,0:T(8,128)(2,1)S(1)} %bitcast.9, bf16[512,512]{1,0:T(8,128)(2,1)S(1)} %bitcast.11), custom_call_target="tpu_custom_call" | custom-call | flops 1073741824 | bytes 4194304 | tf_op jit(solution)/shard_map/near_own/pallas_call | solution.py:255
  70.1 0.0 copy-start.5
  70.1 1.1 copy-done.5
  71.2 0.0 copy-start.7
  71.2 0.7 copy-done.7
  71.8 2.1 %collective-permute-start = (bf16[512,1024]{1,0:T(8,128)(2,1)S(1)}, bf16[512,1024]{1,0:T(8,128)(2,1)S(1)}, u32[]{:S(2)}, u32[]{:S(2)}) collective-permute-start(bf16[512,1024]{1,0:T(8,128)(2,1)S(1)} %get-tuple-element.12), channel_id=1, source_target_pairs={{0,16},{16,32},{32,48},{48,64},{64,80},{80,96},{96,112},{112,128},... | collective-permute-start | bytes 3145736 | tf_op jit(solution)/shard_map/ppermute | solution.py:310
  73.9 0.0 collective-permute-done.1.s01_ref
  73.9 0.0 collective-permute-done.3.s11_ref
  73.9 15.1 %far.1 = bf16[16,72,256]{2,1,0:T(8,128)(2,1)} custom-call(s32[2]{0:T(128)S(1)} %pad_add_fusion.where_ref, bf16[16,72,256]{2,1,0:T(8,128)(2,1)S(1)} %all-to-all-done.got_ref.q_ref, bf16[16,64,128]{2,1,0:T(8,128)(2,1)S(1)} %all_to_all.15.s00_ref, bf16[16,64,128]{2,1,0:T(8,128)(2,1)} %collective-permute-done.1.s01_ref, ...), custom_call_target="tpu_custom_call" | custom-call | flops 5368709120 | bytes 3145728 | tf_op jit(solution)/shard_map/far/pallas_call | solution.py:312
  89.0 4.6 %all-to-all-start.2 = ((bf16[16,72,256]{2,1,0:T(8,128)(2,1)}), bf16[16,72,256]{2,1,0:T(8,128)(2,1)S(1)}, u32[]{:S(2)}, u32[]{:S(2)}) async-start(bf16[16,72,256]{2,1,0:T(8,128)(2,1)} %far.1), calls=%async_computation.2 | async-start | bytes 1179648 | tf_op jit(solution)/shard_map/all_to_all | solution.py:328
  93.6 7.1 %collective-permute-done.rest_0_ = bf16[512,1024]{1,0:T(8,128)(2,1)S(1)} collective-permute-done((bf16[512,1024]{1,0:T(8,128)(2,1)S(1)}, bf16[512,1024]{1,0:T(8,128)(2,1)S(1)}, u32[]{:S(2)}, u32[]{:S(2)}) %collective-permute-start) | collective-permute-done | bytes 1048608 | tf_op jit(solution)/shard_map/ppermute | solution.py:310
  100.7 0.0 copy-start.3
  100.7 1.0 copy-done.3
  101.6 0.0 copy-start.4
  101.6 1.2 %copy-done.4 = bf16[512,1024]{1,0:T(8,128)(2,1)S(1)} copy-done((bf16[512,1024]{1,0:T(8,128)(2,1)S(1)}, bf16[512,1024]{1,0:T(8,128)(2,1)}, u32[]{:S(2)}) %copy-start.4) | copy-done | bytes 1048600
  102.8 0.0 copy-start.6
  102.8 1.3 %copy-done.6 = f32[8,80,512]{2,1,0:T(8,128)S(1)} copy-done((f32[8,80,512]{2,1,0:T(8,128)S(1)}, f32[8,80,512]{2,1,0:T(8,128)}, u32[]{:S(2)}) %copy-start.6) | copy-done | bytes 1310744
  104.2 0.0 copy-start.8
  104.2 0.9 copy-done.8
  105.1 5.2 %near_prev.1 = (f32[8,80,512]{2,1,0:T(8,128)S(1)}, f32[8,8,512]{2,1,0:T(8,128)S(1)}) custom-call(s32[1]{0:T(128)} %bitcast.has_ref, bf16[16,72,256]{2,1,0:T(8,128)(2,1)S(1)} %copy-done, bf16[512,1024]{1,0:T(8,128)(2,1)S(1)} %copy-done.4, f32[8,80,512]{2,1,0:T(8,128)S(1)} %copy-done.6, f32[8,8,512]{2,1,0:T(8,128)S(1)} %copy-done.8), custom_call_target="tpu_custom_call" | custom-call | flops 1073741824 | bytes 4194304 | tf_op jit(solution)/shard_map/near_prev/pallas_call | solution.py:255
  110.3 0.0 all-to-all-done.2.far_ref
  110.3 1.1 %merge.1 = bf16[512,512]{1,0:T(8,128)(2,1)} custom-call(f32[8,80,512]{2,1,0:T(8,128)S(1)} %get-tuple-element.15.acc_ref, f32[8,8,512]{2,1,0:T(8,128)S(1)} %get-tuple-element.16.peak_ref, bf16[16,72,256]{2,1,0:T(8,128)(2,1)S(1)} %all-to-all-done.2.far_ref), custom_call_target="tpu_custom_call" | custom-call | flops 2097152 | bytes 3145728 | tf_op jit(solution)/shard_map/merge/pallas_call | solution.py:331
Async XLA Ops:
  2.5 64.4 %copy-start = (bf16[16,72,256]{2,1,0:T(8,128)(2,1)S(1)}, bf16[16,72,256]{2,1,0:T(8,128)(2,1)}, u32[]{:S(2)}) copy-start(bf16[16,72,256]{2,1,0:T(8,128)(2,1)} %prep.1.qt_ref) | copy-start | bytes 1769476
  2.5 64.4 %copy-start.1 = (bf16[1,512,512]{2,1,0:T(8,128)(2,1)S(1)}, bf16[1,512,512]{2,1,0:T(8,128)(2,1)}, u32[]{:S(2)}) copy-start(bf16[1,512,512]{2,1,0:T(8,128)(2,1)} %param.5) | copy-start | bytes 1572868
  2.5 64.4 %copy-start.2 = (bf16[1,512,512]{2,1,0:T(8,128)(2,1)S(1)}, bf16[1,512,512]{2,1,0:T(8,128)(2,1)}, u32[]{:S(2)}) copy-start(bf16[1,512,512]{2,1,0:T(8,128)(2,1)} %param.6) | copy-start | bytes 1572868
  2.5 22.4 %all-to-all-start = ((bf16[16,72,256]{2,1,0:T(8,128)(2,1)}), bf16[16,72,256]{2,1,0:T(8,128)(2,1)S(1)}, u32[]{:S(2)}, u32[]{:S(2)}) async-start(bf16[16,72,256]{2,1,0:T(8,128)(2,1)} %prep.1.qt_ref), calls=%async_computation | async-start | bytes 1179648 | tf_op jit(solution)/shard_map/all_to_all | solution.py:293
  54.3 9.5 %collective-permute-start.2 = (bf16[16,64,128]{2,1,0:T(8,128)(2,1)S(1)}, bf16[16,64,128]{2,1,0:T(8,128)(2,1)}, u32[]{:S(2)}, u32[]{:S(2)}) collective-permute-start(bf16[16,64,128]{2,1,0:T(8,128)(2,1)S(1)} %all_to_all.15.s00_ref), channel_id=1, source_target_pairs={{0,256},{16,272},{32,288},{48,304},{64,320},{80,336},{96,352},{112... | collective-permute-start | bytes 786440 | tf_op jit(solution)/shard_map/ppermute | solution.py:304
  56.6 17.3 %collective-permute-start.1 = (bf16[16,64,128]{2,1,0:T(8,128)(2,1)S(1)}, bf16[16,64,128]{2,1,0:T(8,128)(2,1)}, u32[]{:S(2)}, u32[]{:S(2)}) collective-permute-start(bf16[16,64,128]{2,1,0:T(8,128)(2,1)S(1)} %all_to_all.15.s00_ref), channel_id=1, source_target_pairs={{0,1},{1,0},{2,3},{3,2},{4,5},{5,4},{6,7},{7,6},{8,9},{9,8},{10,11... | collective-permute-start | bytes 786440 | tf_op jit(solution)/shard_map/ppermute | solution.py:305
  63.7 10.2 %collective-permute-start.3 = (bf16[16,64,128]{2,1,0:T(8,128)(2,1)}, bf16[16,64,128]{2,1,0:T(8,128)(2,1)}, u32[]{:S(2)}, u32[]{:S(2)}) collective-permute-start(bf16[16,64,128]{2,1,0:T(8,128)(2,1)} %collective-permute-done.2.s10_ref), channel_id=1, source_target_pairs={{0,1},{1,0},{2,3},{3,2},{4,5},{5,4},{6,7},{7,6},{8,9},{9,8},{10,11... | collective-permute-start | bytes 786440 | tf_op jit(solution)/shard_map/ppermute | solution.py:306
  70.1 1.1 copy-start.5
  71.2 0.7 copy-start.7
  71.8 28.8 %collective-permute-start = (bf16[512,1024]{1,0:T(8,128)(2,1)S(1)}, bf16[512,1024]{1,0:T(8,128)(2,1)S(1)}, u32[]{:S(2)}, u32[]{:S(2)}) collective-permute-start(bf16[512,1024]{1,0:T(8,128)(2,1)S(1)} %get-tuple-element.12), channel_id=1, source_target_pairs={{0,16},{16,32},{32,48},{48,64},{64,80},{80,96},{96,112},{112,128},... | collective-permute-start | bytes 3145736 | tf_op jit(solution)/shard_map/ppermute | solution.py:310
  89.0 21.3 %all-to-all-start.2 = ((bf16[16,72,256]{2,1,0:T(8,128)(2,1)}), bf16[16,72,256]{2,1,0:T(8,128)(2,1)S(1)}, u32[]{:S(2)}, u32[]{:S(2)}) async-start(bf16[16,72,256]{2,1,0:T(8,128)(2,1)} %far.1), calls=%async_computation.2 | async-start | bytes 1179648 | tf_op jit(solution)/shard_map/all_to_all | solution.py:328
  100.7 1.0 copy-start.3
  101.6 1.2 %copy-start.4 = (bf16[512,1024]{1,0:T(8,128)(2,1)S(1)}, bf16[512,1024]{1,0:T(8,128)(2,1)}, u32[]{:S(2)}) copy-start(bf16[512,1024]{1,0:T(8,128)(2,1)} %copy-done.3) | copy-start | bytes 3145732
  102.8 1.3 %copy-start.6 = (f32[8,80,512]{2,1,0:T(8,128)S(1)}, f32[8,80,512]{2,1,0:T(8,128)}, u32[]{:S(2)}) copy-start(f32[8,80,512]{2,1,0:T(8,128)} %copy-done.5) | copy-start | bytes 3932164
  104.2 0.9 copy-start.8
